TPU v7x, 32 devices: a whole 2x2x4 slice. The times are simulated.
32 devices in a mesh: dp: 16 (over z, y, core), tensor: 2 (over x).
Axes of the slice: x: 2, y: 2, z: 4, core: 2. Of those that a mesh axis runs over, the one named last changes fastest.
Arguments:
- h_in: bfloat16 [16, 2, 512, 768], P('dp', None, 'tensor'), may hold values from -6 to 6
- g_in: bfloat16 [16, 2, 512, 768], P('dp', None, 'tensor'), may hold values from -6 to 6
- mem_in: bfloat16 [16, 2, 384, 768], P('dp', None, 'tensor'), may hold values from -6 to 6
- d_h_out: bfloat16 [16, 2, 512, 768], P('dp', None, 'tensor'), may hold values from -6 to 6
- d_g_out: bfloat16 [16, 2, 512, 768], P('dp', None, 'tensor'), may hold values from -6 to 6
- w_query: bfloat16 [768, 768], P(None, 'tensor'), may hold values from -0.21875 to 0.21875
- w_key: bfloat16 [768, 768], P(None, 'tensor'), may hold values from -0.21875 to 0.21875
- w_value: bfloat16 [768, 768], P(None, 'tensor'), may hold values from -0.21875 to 0.21875
- w_out: bfloat16 [768, 768], P('tensor'), may hold values from -0.875 to 0.875
- content_bias: float32 [12, 64], P('tensor'), may hold values from -3 to 3
- seg_bias: float32 [12, 64], P('tensor'), may hold values from -3 to 3
- seg_embed: float32 [2, 12, 64], P(None, 'tensor'), may hold values from -6 to 6
- rel_table: float32 [12, 32], P('tensor'), may hold values from -48 to 48
- norm1_gain: float32 [768], replicated, may hold values from 0.5 to 1.5
- norm1_bias: float32 [768], replicated, may hold values from -1.2 to 1.2
- w_in: bfloat16 [768, 3072], P(None, 'tensor'), may hold values from -0.21875 to 0.21875
- b_in: float32 [3072], P('tensor'), may hold values from -1.8 to 1.8
- w_ffo: bfloat16 [3072, 768], P('tensor'), may hold values from -0.109375 to 0.109375
- b_ffo: float32 [768], replicated, may hold values from -1.2 to 1.2
- norm2_gain: float32 [768], replicated, may hold values from 0.5 to 1.5
- norm2_bias: float32 [768], replicated, may hold values from -1.2 to 1.2
- bucket_len: int32 [16, 2], P('dp'), may hold values from 64 to 512, as said below
- doc_len: int32 [16, 2, 8], P('dp'), may hold values from 0 to 512, as said below
- seg_ids: int32 [16, 2, 512], P('dp'), may hold values from 0 to 1
- mem_seg: int32 [16, 2, 384], P('dp'), may hold values from 0 to 1
- perm_rank: int32 [16, 2, 512], P('dp'), may hold values from 0 to 63
Outputs:
- h_out: bfloat16 [16, 2, 512, 768], P('dp', None, 'tensor')
- g_out: bfloat16 [16, 2, 512, 768], P('dp', None, 'tensor')
- d_h_in: bfloat16 [16, 2, 512, 768], P('dp', None, 'tensor')
- d_g_in: bfloat16 [16, 2, 512, 768], P('dp', None, 'tensor')
- d_mem_in: bfloat16 [16, 2, 384, 768], P('dp', None, 'tensor')
- d_w_query: float32 [768, 768], P(None, 'tensor')
- d_w_key: float32 [768, 768], P(None, 'tensor')
- d_w_value: float32 [768, 768], P(None, 'tensor')
- d_w_out: float32 [768, 768], P('tensor')
- d_content_bias: float32 [12, 64], P('tensor')
- d_seg_bias: float32 [12, 64], P('tensor')
- d_seg_embed: float32 [2, 12, 64], P(None, 'tensor')
- d_rel_table: float32 [12, 32], P('tensor')
- d_norm1_gain: float32 [768], replicated
- d_norm1_bias: float32 [768], replicated
- d_w_in: float32 [768, 3072], P(None, 'tensor')
- d_b_in: float32 [3072], P('tensor')
- d_w_ffo: float32 [3072, 768], P('tensor')
- d_b_ffo: float32 [768], replicated
- d_norm2_gain: float32 [768], replicated
- d_norm2_bias: float32 [768], replicated
Inputs may be any that keep to these rules, and one draw needn't show every extreme that they name: `bucket_len`: every entry is 512, 256, 128 or 64; counting slots group by group, the first slot of all is 512 and the second 512 // 8. `doc_len`: for a slot whose bucket_len is b, entry k is 0 when k * b >= 512, else between b // 2 and b; entry 0 equals b.
All inputs are finite; a program needn't handle non-finite values.
Results may differ from a plain program's by a relative error of at most 0.03.
Values may be sent and summed in bfloat16 or wider, within the bound.
No kernel may reach another device: no remote copies, remote signals or barrier semaphores. Data moves between devices by JAX's collectives and lax.ppermute only.
A program may use at most 320 MiB of HBM per device.

v0:
```python
from functools import partial

import jax
import jax.numpy as jnp
from jax import lax
from jax.sharding import PartitionSpec as P

HDIM = 64
NREL = 32


epsilon = 1e-05
masked_score = -1e30
target_floor = 48
distance_steps = (1, 2, 3, 4, 5, 6, 7, 8, 12, 16, 24, 32, 64, 128, 256)
highest = lax.Precision.HIGHEST


def bucket_of(distance):
    magnitude = jnp.abs(distance)
    counted = jnp.zeros(distance.shape, jnp.int32)
    for threshold in distance_steps:
        counted = counted + (magnitude >= threshold).astype(jnp.int32)
    return counted + NREL // 2 * (distance > 0).astype(jnp.int32)


def slot_masks(bucket, doc_len, perm_rank, seg_ids, mem_seg):
    slot_rows = perm_rank.shape[0]
    mem_rows = mem_seg.shape[0]
    positions = jnp.arange(slot_rows, dtype=jnp.int32)
    document = positions // bucket
    within = positions - document * bucket
    doc_index = jnp.arange(doc_len.shape[0], dtype=jnp.int32)
    doc_length = jnp.sum(
        jnp.where(document[:, None] == doc_index[None, :], doc_len[None, :], 0),
        axis=1,
        dtype=jnp.int32,
    )
    present = within < doc_length
    factor_order = jnp.where(within < 2, 0, jnp.maximum(perm_rank - target_floor, 0))
    same_doc = (document[:, None] == document[None, :]) & present[None, :]
    itself = positions[:, None] == positions[None, :]
    content_see = same_doc & (factor_order[None, :] <= factor_order[:, None]) | itself
    query_see = (
        same_doc
        & jnp.logical_not(itself)
        & ((factor_order[None, :] < factor_order[:, None]) | (factor_order[None, :] == 0))
    )
    memory_see = jnp.broadcast_to(bucket == slot_rows, (slot_rows, mem_rows))
    see_content = jnp.concatenate([memory_see, content_see], axis=1)
    see_query = jnp.concatenate([memory_see, query_see], axis=1)
    key_place = jnp.concatenate([jnp.arange(mem_rows, dtype=jnp.int32) - mem_rows, positions])
    buckets = bucket_of(positions[:, None] - key_place[None, :])
    same_seg = seg_ids[:, None] == jnp.concatenate([mem_seg, seg_ids])[None, :]
    return (see_content, see_query, buckets, same_seg)


def layer_norm(values_in, norm_gain, norm_bias):
    centred = values_in - jnp.mean(values_in, axis=-1, keepdims=True)
    spread = jnp.mean(centred * centred, axis=-1, keepdims=True)
    return centred * lax.rsqrt(spread + epsilon) * norm_gain + norm_bias


def score_block(queries, key_rows, visible, rel_slot, same_seg, small_params):
    content_bias, seg_bias, seg_embed, rel_table = small_params
    scores = jnp.einsum("ihd,jhd->hij", queries, key_rows, preferred_element_type=jnp.float32)
    key_shift = jnp.einsum(
        "hd,jhd->hj", content_bias, key_rows.astype(jnp.float32), precision=highest
    )
    seg_terms = jnp.einsum(
        "ihd,chd->chi", queries.astype(jnp.float32) + seg_bias[None], seg_embed, precision=highest
    )
    scores = scores + key_shift[:, None, :]
    scores = scores + jnp.where(same_seg[None], seg_terms[1][:, :, None], seg_terms[0][:, :, None])
    scores = scores + rel_slot
    return jnp.where(visible[None], scores * HDIM ** (-0.5), masked_score)


def attend_forward(queries, key_rows, value_rows, visible, rel_slot, same_seg, small_params):
    scores = score_block(queries, key_rows, visible, rel_slot, same_seg, small_params)
    row_max = jnp.max(scores, axis=-1, keepdims=True)
    exponent = jnp.exp(scores - row_max)
    row_total = jnp.sum(exponent, axis=-1, keepdims=True)
    weights = (exponent / row_total).astype(jnp.bfloat16)
    attended = jnp.einsum("hij,jhd->ihd", weights, value_rows, preferred_element_type=jnp.float32)
    return (
        attended.reshape(attended.shape[0], -1).astype(jnp.bfloat16),
        (row_max + jnp.log(row_total))[:, :, 0],
    )


def attend_backward(
    queries,
    key_rows,
    value_rows,
    visible,
    rel_slot,
    same_seg,
    log_total,
    d_attended,
    small_params,
    one_hot,
):
    content_bias, seg_bias, seg_embed, rel_table = small_params
    score_scale = HDIM ** (-0.5)
    scores = score_block(queries, key_rows, visible, rel_slot, same_seg, small_params)
    weights = jnp.exp(scores - log_total[:, :, None])
    d_weights = jnp.einsum(
        "ihd,jhd->hij", d_attended, value_rows, preferred_element_type=jnp.float32
    )
    d_value = jnp.einsum(
        "hij,ihd->jhd", weights.astype(jnp.bfloat16), d_attended, preferred_element_type=jnp.float32
    )
    inner_sum = jnp.sum(weights * d_weights, axis=-1, keepdims=True)
    d_scores = (weights * (d_weights - inner_sum)).astype(jnp.bfloat16)
    scaled_grad = d_scores.astype(jnp.float32) * score_scale
    d_query = (
        jnp.einsum("hij,jhd->ihd", d_scores, key_rows, preferred_element_type=jnp.float32)
        * score_scale
    )
    d_key = (
        jnp.einsum("hij,ihd->jhd", d_scores, queries, preferred_element_type=jnp.float32)
        * score_scale
    )
    column = jnp.sum(scaled_grad, axis=1)
    d_key = d_key + column.T[:, :, None] * content_bias[None]
    d_content_bias = jnp.einsum(
        "hj,jhd->hd", column, key_rows.astype(jnp.float32), precision=highest
    )
    same_part = jnp.sum(jnp.where(same_seg[None], scaled_grad, 0.0), axis=-1)
    other_part = jnp.sum(jnp.where(same_seg[None], 0.0, scaled_grad), axis=-1)
    d_seg = jnp.stack([other_part, same_part])
    d_query = d_query + jnp.einsum("chi,chd->ihd", d_seg, seg_embed, precision=highest)
    d_seg_bias = jnp.einsum("chi,chd->hd", d_seg, seg_embed, precision=highest)
    d_seg_embed = jnp.einsum(
        "chi,ihd->chd", d_seg, queries.astype(jnp.float32) + seg_bias[None], precision=highest
    )
    d_table = (
        jnp.einsum("hij,rij->hr", d_scores, one_hot, preferred_element_type=jnp.float32)
        * score_scale
    )
    return (d_query, d_key, d_value, (d_content_bias, d_seg_bias, d_seg_embed, d_table))


def per_device(
    h_in,
    g_in,
    mem_in,
    d_h_out,
    d_g_out,
    w_query,
    w_key,
    w_value,
    w_out,
    content_bias,
    seg_bias,
    seg_embed,
    rel_table,
    norm1_gain,
    norm1_bias,
    w_in,
    b_in,
    w_ffo,
    b_ffo,
    norm2_gain,
    norm2_bias,
    bucket_len,
    doc_len,
    seg_ids,
    mem_seg,
    perm_rank,
):
    mem_rows = mem_seg.shape[2]
    content_local, stream_local, memory_local, cot_content, cot_stream = (
        h_in[0],
        g_in[0],
        mem_in[0],
        d_h_out[0],
        d_g_out[0],
    )
    slot_ints = (bucket_len[0], doc_len[0], perm_rank[0], seg_ids[0], mem_seg[0])
    head_local = w_query.shape[1] // HDIM
    pair_local = jnp.stack([content_local, stream_local], axis=1)
    see_content, see_query, buckets, same_seg = jax.vmap(slot_masks)(*slot_ints)
    visible_pair = jnp.stack([see_content, see_query], axis=1)
    small_params = (content_bias, seg_bias, seg_embed, rel_table)
    rel_ids = jnp.arange(NREL, dtype=jnp.int32)

    def slot_bias(bucket_slot):
        one_hot = (bucket_slot[None] == rel_ids[:, None, None]).astype(jnp.float32)
        return jnp.einsum("hr,rij->hij", rel_table, one_hot, precision=highest)

    rel_bias = lax.map(slot_bias, buckets)

    def split_heads(values_in):
        return values_in.reshape(values_in.shape[:-1] + (head_local, HDIM))

    def forward_pass(pair_input, memory_input):
        pair_all, memory_all = (
            lax.all_gather(pair_input, "tensor", axis=2, tiled=True),
            lax.all_gather(memory_input, "tensor", axis=1, tiled=True),
        )
        key_input = jnp.concatenate([memory_all, pair_all[:, 0]], axis=1)
        key_rows = jnp.dot(key_input, w_key, preferred_element_type=jnp.float32).astype(
            jnp.bfloat16
        )
        value_rows = jnp.dot(key_input, w_value, preferred_element_type=jnp.float32).astype(
            jnp.bfloat16
        )
        query_pair = jnp.dot(pair_all, w_query, preferred_element_type=jnp.float32).astype(
            jnp.bfloat16
        )

        def attend_slot(slot_items):
            queries, key_slot, value_slot, visible, rel_slot, seg_slot = slot_items
            results = [
                attend_forward(
                    split_heads(queries[stream]),
                    split_heads(key_slot),
                    split_heads(value_slot),
                    visible[stream],
                    rel_slot,
                    seg_slot,
                    small_params,
                )
                for stream in range(2)
            ]
            return (
                jnp.stack([results[0][0], results[1][0]]),
                jnp.stack([results[0][1], results[1][1]]),
            )

        attended, log_total = lax.map(
            attend_slot, (query_pair, key_rows, value_rows, visible_pair, rel_bias, same_seg)
        )
        projected = jnp.dot(attended, w_out, preferred_element_type=jnp.float32)
        attn_local = lax.psum_scatter(
            projected.astype(jnp.bfloat16), "tensor", scatter_dimension=2, tiled=True
        ).astype(jnp.float32)
        mid_rows = pair_input.astype(jnp.float32) + attn_local
        normed = layer_norm(mid_rows, norm1_gain, norm1_bias)
        ffn_input = lax.all_gather(normed.astype(jnp.bfloat16), "tensor", axis=2, tiled=True)
        hidden = jnp.dot(ffn_input, w_in, preferred_element_type=jnp.float32) + b_in
        active = jax.nn.gelu(hidden, approximate=True).astype(jnp.bfloat16)
        ffn_part = jnp.dot(active, w_ffo, preferred_element_type=jnp.float32)
        ffn_local = lax.psum_scatter(
            ffn_part.astype(jnp.bfloat16), "tensor", scatter_dimension=2, tiled=True
        ).astype(jnp.float32)
        second = normed + ffn_local + b_ffo
        return {
            "pair_all": pair_all,
            "key_input": key_input,
            "key_rows": key_rows,
            "value_rows": value_rows,
            "query_pair": query_pair,
            "attended": attended,
            "log_total": log_total,
            "mid_rows": mid_rows,
            "ffn_input": ffn_input,
            "hidden": hidden,
            "active": active,
            "second": second,
        }

    stored = forward_pass(pair_local, memory_local)
    outputs = layer_norm(stored["second"], norm2_gain, norm2_bias)
    pair_again, memory_again, outputs = lax.optimization_barrier(
        (pair_local, memory_local, outputs)
    )
    stored = forward_pass(pair_again, memory_again)
    cot_pair = jnp.stack([cot_content, cot_stream], axis=1).astype(jnp.float32)
    norm2_pull = jax.vjp(layer_norm, stored["second"], norm2_gain, norm2_bias)[1]
    d_second, d_norm2_gain, d_norm2_bias = norm2_pull(cot_pair)
    d_ffn = d_second.astype(jnp.bfloat16)
    d_b_ffo = jnp.sum(d_ffn.astype(jnp.float32), axis=(0, 1, 2))
    d_ffn_all = lax.all_gather(d_ffn, "tensor", axis=2, tiled=True)
    d_w_ffo = jnp.einsum(
        "sqif,sqid->fd", stored["active"], d_ffn_all, preferred_element_type=jnp.float32
    )
    d_active = jnp.einsum("sqid,fd->sqif", d_ffn_all, w_ffo, preferred_element_type=jnp.float32)
    gelu_pull = jax.vjp(partial(jax.nn.gelu, approximate=True), stored["hidden"])[1]
    d_hidden = gelu_pull(d_active)[0].astype(jnp.bfloat16)
    d_b_in = jnp.sum(d_hidden.astype(jnp.float32), axis=(0, 1, 2))
    d_w_in = jnp.einsum(
        "sqid,sqif->df", stored["ffn_input"], d_hidden, preferred_element_type=jnp.float32
    )
    normed_part = jnp.einsum("sqif,df->sqid", d_hidden, w_in, preferred_element_type=jnp.float32)
    d_normed = d_second + lax.psum_scatter(
        normed_part.astype(jnp.bfloat16), "tensor", scatter_dimension=2, tiled=True
    ).astype(jnp.float32)
    norm1_pull = jax.vjp(layer_norm, stored["mid_rows"], norm1_gain, norm1_bias)[1]
    d_mid, d_norm1_gain, d_norm1_bias = norm1_pull(d_normed)
    d_attn_all = lax.all_gather(d_mid.astype(jnp.bfloat16), "tensor", axis=2, tiled=True)
    d_w_out = jnp.einsum(
        "sqie,sqid->ed", stored["attended"], d_attn_all, preferred_element_type=jnp.float32
    )
    d_attended = jnp.einsum(
        "sqid,ed->sqie", d_attn_all, w_out, preferred_element_type=jnp.float32
    ).astype(jnp.bfloat16)

    def attend_slot_back(slot_items):
        (
            queries,
            key_slot,
            value_slot,
            visible,
            bucket_slot,
            rel_slot,
            seg_slot,
            log_slot,
            d_slot,
        ) = slot_items
        one_hot = (bucket_slot[None] == rel_ids[:, None, None]).astype(jnp.bfloat16)
        key_heads = split_heads(key_slot)
        value_heads = split_heads(value_slot)
        query_grads = []
        d_key_sum = jnp.zeros(key_heads.shape, jnp.float32)
        d_value_sum = jnp.zeros(value_heads.shape, jnp.float32)
        small_sum = tuple((jnp.zeros_like(member) for member in small_params))
        for stream in range(2):
            d_query, d_key, d_value, small_grads = attend_backward(
                split_heads(queries[stream]),
                key_heads,
                value_heads,
                visible[stream],
                rel_slot,
                seg_slot,
                log_slot[stream],
                split_heads(d_slot[stream]),
                small_params,
                one_hot,
            )
            query_grads.append(d_query.reshape(d_query.shape[0], -1).astype(jnp.bfloat16))
            d_key_sum = d_key_sum + d_key
            d_value_sum = d_value_sum + d_value
            small_sum = jax.tree.map(jnp.add, small_sum, small_grads)
        key_width = d_key_sum.shape[0]
        return (
            jnp.stack(query_grads),
            d_key_sum.reshape(key_width, -1).astype(jnp.bfloat16),
            d_value_sum.reshape(key_width, -1).astype(jnp.bfloat16),
            small_sum,
        )

    d_query_pair, d_key_rows, d_value_rows, slot_smalls = lax.map(
        attend_slot_back,
        (
            stored["query_pair"],
            stored["key_rows"],
            stored["value_rows"],
            visible_pair,
            buckets,
            rel_bias,
            same_seg,
            stored["log_total"],
            d_attended,
        ),
    )
    d_content_bias = jnp.sum(slot_smalls[0], axis=0)
    d_seg_bias = jnp.sum(slot_smalls[1], axis=0)
    d_seg_embed = jnp.sum(slot_smalls[2], axis=0)
    d_rel_table = jnp.sum(slot_smalls[3], axis=0)
    d_w_query = jnp.einsum(
        "sqid,sqie->de", stored["pair_all"], d_query_pair, preferred_element_type=jnp.float32
    )
    d_w_key = jnp.einsum(
        "sjd,sje->de", stored["key_input"], d_key_rows, preferred_element_type=jnp.float32
    )
    d_w_value = jnp.einsum(
        "sjd,sje->de", stored["key_input"], d_value_rows, preferred_element_type=jnp.float32
    )
    d_pair_part = jnp.einsum(
        "sqie,de->sqid", d_query_pair, w_query, preferred_element_type=jnp.float32
    )
    d_key_part = jnp.einsum(
        "sje,de->sjd", d_key_rows, w_key, preferred_element_type=jnp.float32
    ) + jnp.einsum("sje,de->sjd", d_value_rows, w_value, preferred_element_type=jnp.float32)
    d_pair_part = jnp.concatenate(
        [(d_pair_part[:, 0] + d_key_part[:, mem_rows:])[:, None], d_pair_part[:, 1:]], axis=1
    )
    d_pair_local, d_memory = (
        lax.psum_scatter(
            d_pair_part.astype(jnp.bfloat16), "tensor", scatter_dimension=2, tiled=True
        ).astype(jnp.float32),
        lax.psum_scatter(
            d_key_part[:, :mem_rows].astype(jnp.bfloat16), "tensor", scatter_dimension=1, tiled=True
        ).astype(jnp.float32),
    )
    d_pair_local = d_pair_local + d_mid
    norm_sums = lax.psum(
        (d_norm1_gain, d_norm1_bias, d_norm2_gain, d_norm2_bias, d_b_ffo), ("dp", "tensor")
    )
    weight_terms = (
        d_w_query,
        d_w_key,
        d_w_value,
        d_w_out,
        d_content_bias,
        d_seg_bias,
        d_seg_embed,
        d_rel_table,
        d_w_in,
        d_b_in,
        d_w_ffo,
    )
    all_sums = lax.psum(
        (
            weight_terms[0],
            weight_terms[1],
            weight_terms[2],
            weight_terms[3],
            weight_terms[4],
            weight_terms[5],
            weight_terms[6],
            weight_terms[7],
            weight_terms[8],
            weight_terms[9],
            weight_terms[10],
        ),
        "dp",
    )
    results = (
        outputs[:, 0].astype(jnp.bfloat16),
        outputs[:, 1].astype(jnp.bfloat16),
        d_pair_local[:, 0].astype(jnp.bfloat16),
        d_pair_local[:, 1].astype(jnp.bfloat16),
        d_memory.astype(jnp.bfloat16),
    )
    return (
        results[0][None],
        results[1][None],
        results[2][None],
        results[3][None],
        results[4][None],
        all_sums[0],
        all_sums[1],
        all_sums[2],
        all_sums[3],
        all_sums[4],
        all_sums[5],
        all_sums[6],
        all_sums[7],
        norm_sums[0],
        norm_sums[1],
        all_sums[8],
        all_sums[9],
        all_sums[10],
        norm_sums[4],
        norm_sums[2],
        norm_sums[3],
    )


def solution(mesh):
    return jax.shard_map(
        per_device,
        mesh=mesh,
        in_specs=(
            P("dp", None, "tensor", None),
            P("dp", None, "tensor", None),
            P("dp", None, "tensor", None),
            P("dp", None, "tensor", None),
            P("dp", None, "tensor", None),
            P(None, "tensor"),
            P(None, "tensor"),
            P(None, "tensor"),
            P("tensor", None),
            P("tensor", None),
            P("tensor", None),
            P(None, "tensor", None),
            P("tensor", None),
            P(),
            P(),
            P(None, "tensor"),
            P("tensor"),
            P("tensor", None),
            P(),
            P(),
            P(),
            P("dp", None),
            P("dp", None, None),
            P("dp", None, None),
            P("dp", None, None),
            P("dp", None, None),
        ),
        out_specs=(
            P("dp", None, "tensor", None),
            P("dp", None, "tensor", None),
            P("dp", None, "tensor", None),
            P("dp", None, "tensor", None),
            P("dp", None, "tensor", None),
            P(None, "tensor"),
            P(None, "tensor"),
            P(None, "tensor"),
            P("tensor", None),
            P("tensor", None),
            P("tensor", None),
            P(None, "tensor", None),
            P("tensor", None),
            P(),
            P(),
            P(None, "tensor"),
            P("tensor"),
            P("tensor", None),
            P(),
            P(),
            P(),
        ),
        check_vma=False,
    )
```

profile of v0, /device:TPU:0, one launch (start us, length us, event | category | flops | bytes accessed | tf_op | source)
XLA Modules:
  0.0 1581.5 jit_solution(2160015649002116654)
XLA Ops:
  18.1 67.0 %while.58 = (s32[]{:T(128)}, f32[2,6,512,896]{3,2,1,0:T(8,128)}, s32[2,512,896]{2,1,0:T(8,128)}, f32[6,32]{1,0:T(8,128)S(1)}, s32[]{:T(128)}) while((s32[]{:T(128)}, f32[2,6,512,896]{3,2,1,0:T(8,128)}, s32[2,512,896]{2,1,0:T(8,128)}, f32[6,32]{1,0:T(8,128)S(1)}, s32[]{:T(128)}) %tuple.244), condition=%wide.region_2.3_spmd.clone, body=%wide.region_1.2_spmd.clone.sunk | while | flops 1071644672 | bytes 42206028 | solution.py:193
  20.5 20.1 %fusion.491 = f32[1,6,512,896]{3,1,2,0:T(8,128)} fusion(s32[512,896]{1,0:T(8,128)S(1)} %dynamic-slice_bitcast_fusion.26, f32[6,32]{1,0:T(8,128)S(1)} %get-tuple-element.1102), kind=kOutput, calls=%fused_computation.92.clone.1 | convolution fusion | flops 1071644672 | bytes 12845824 | tf_op jit(solution)/shard_map/while/body/eval_jaxpr/hr,rij->hij/dot_general | solution.py:191
  40.6 11.5 copy_dynamic-update-slice_fusion.2
  53.7 20.1 %fusion.491 = f32[1,6,512,896]{3,1,2,0:T(8,128)} fusion(s32[512,896]{1,0:T(8,128)S(1)} %dynamic-slice_bitcast_fusion.26, f32[6,32]{1,0:T(8,128)S(1)} %get-tuple-element.1102), kind=kOutput, calls=%fused_computation.92.clone.1 | convolution fusion | flops 1071644672 | bytes 12845824 | tf_op jit(solution)/shard_map/while/body/eval_jaxpr/hr,rij->hij/dot_general | solution.py:191
  73.8 11.3 copy_dynamic-update-slice_fusion.2
  109.3 162.3 %while.56 = (s32[]{:T(128)}, bf16[2,2,512,384]{2,3,0,1:T(8,128)(2,1)}, bf16[2,896,384]{2,1,0:T(8,128)(2,1)}, pred[2,2,512,896]{3,2,1,0:T(8,128)(4,1)}, bf16[2,2,...) while((s32[]{:T(128)}, ...), condition=%wide.region_8.9_spmd, body=%wide.region_3.8_spmd.sunk | while | flops 1486169600 | bytes 118329104 | solution.py:233
  128.2 9.0 fusion.463
  137.3 10.0 fusion.464
  147.2 11.3 fusion.465
  158.5 9.0 fusion.459
  167.5 9.4 fusion.460
  176.9 11.3 fusion.461
  209.1 9.0 fusion.463
  218.2 10.0 fusion.464
  228.1 11.3 fusion.465
  248.4 9.4 fusion.460
  257.8 11.3 fusion.461
  276.7 46.3 %reduce-scatter.8.cloned.1.call-done = bf16[2,2,256,768]{3,2,0,1:T(8,128)(2,1)} async-done(((bf16[2,2,512,768]{3,2,0,1:T(8,128)(2,1)}), bf16[2,2,256,768]{3,2,0,1:T(8,128)(2,1)}) %reduce-scatter.8.cloned.1.call-update) | async-done | bytes 1572880 | tf_op jit(solution)/shard_map/reduce_scatter | solution.py:237
  328.5 45.0 %all-gather.12.cloned.1.call-done = bf16[2,2,512,768]{3,2,0,1:T(8,128)(2,1)} async-done(((bf16[2,2,256,768]{3,2,0,1:T(8,128)(2,1)}), bf16[2,2,512,768]{3,2,0,1:T(8,128)(2,1)}) %all-gather.12.cloned.1.call-update) | async-done | bytes 3145744 | tf_op jit(solution)/shard_map/all_gather | solution.py:242
  373.5 9.7 fusion.139
  389.6 43.5 %reduce-scatter.10.cloned.1.call-done = bf16[2,2,256,768]{3,2,0,1:T(8,128)(2,1)} async-done(((bf16[2,2,512,768]{3,2,0,1:T(8,128)(2,1)}), bf16[2,2,256,768]{3,2,0,1:T(8,128)(2,1)}) %reduce-scatter.10.cloned.1.call-update) | async-done | bytes 1572880 | tf_op jit(solution)/shard_map/reduce_scatter | solution.py:246
  443.8 44.1 %all-gather.16.cloned.1.call-done = bf16[2,2,512,768]{3,2,0,1:T(8,128)(2,1)} async-done(((bf16[2,2,256,768]{3,2,0,1:T(8,128)(2,1)}), bf16[2,2,512,768]{3,2,0,1:T(8,128)(2,1)}) %all-gather.16.cloned.1.call-update) | async-done | bytes 3145744 | tf_op jit(solution)/shard_map/all_gather | solution.py:200
  490.5 21.7 %all-gather.14.cloned.1.call-done = bf16[2,384,768]{2,1,0:T(8,128)(2,1)} async-done(((bf16[2,192,768]{2,1,0:T(8,128)(2,1)}), bf16[2,384,768]{2,1,0:T(8,128)(2,1)}) %all-gather.14.cloned.1.call-update) | async-done | bytes 1179664 | tf_op jit(solution)/shard_map/all_gather | solution.py:201
  535.2 63.4 %while.57 = (s32[]{:T(128)}, bf16[2,2,512,384]{2,3,0,1:T(8,128)(2,1)}, f32[2,2,6,512]{3,2,1,0:T(8,128)S(1)}, bf16[2,896,384]{1,2,0:T(8,128)(2,1)}, pred[2,2,512,...) while((s32[]{:T(128)}, ...), condition=%wide.region_20.21_spmd, body=%wide.region_15.20_spmd.sunk | while | flops 1491664896 | bytes 135974736 | solution.py:233
  603.7 43.5 %reduce-scatter.12.cloned.1.call-done = bf16[2,2,256,768]{3,2,0,1:T(8,128)(2,1)} async-done(((bf16[2,2,512,768]{3,2,0,1:T(8,128)(2,1)}), bf16[2,2,256,768]{3,2,0,1:T(8,128)(2,1)}) %reduce-scatter.12.cloned.1.call-update) | async-done | bytes 1572880 | tf_op jit(solution)/shard_map/reduce_scatter | solution.py:237
  652.9 45.0 %all-gather.18.cloned.1.call-done = bf16[2,2,512,768]{3,2,0,1:T(8,128)(2,1)} async-done(((bf16[2,2,256,768]{3,2,0,1:T(8,128)(2,1)}), bf16[2,2,512,768]{3,2,0,1:T(8,128)(2,1)}) %all-gather.18.cloned.1.call-update) | async-done | bytes 3145744 | tf_op jit(solution)/shard_map/all_gather | solution.py:242
  697.9 12.3 multiply_convert_fusion.2
  719.3 43.5 %reduce-scatter.14.cloned.1.call-done = bf16[2,2,256,768]{3,2,0,1:T(8,128)(2,1)} async-done(((bf16[2,2,512,768]{3,2,0,1:T(8,128)(2,1)}), bf16[2,2,256,768]{3,2,0,1:T(8,128)(2,1)}) %reduce-scatter.14.cloned.1.call-update) | async-done | bytes 1572880 | tf_op jit(solution)/shard_map/reduce_scatter | solution.py:246
  775.4 45.0 %all-gather.20.cloned.1.call-done = bf16[2,2,512,768]{3,2,0,1:T(8,128)(2,1)} async-done(((bf16[2,2,256,768]{3,2,0,1:T(8,128)(2,1)}), bf16[2,2,512,768]{3,2,0,1:T(8,128)(2,1)}) %all-gather.20.cloned.1.call-update) | async-done | bytes 3145744 | tf_op jit(solution)/shard_map/all_gather | solution.py:276
  820.4 16.8 %convert_reduce_fusion = (f32[1536]{0:T(1024)}, bf16[2,2,512,1536]{3,2,1,0:T(8,128)(2,1)S(1)}) fusion(f32[2,2,512,1536]{3,2,1,0:T(8,128)} %get-tuple-element.678, f32[1536]{0:T(1024)S(1)} %copy-done.90, bf16[1536,768]{1,0:T(8,128)(2,1)} %param.51, bf16[2,2,512,768]{3,2,0,1:T(8,128)(2,1)} %all-gather.20.cloned.1.call-done), kind=kOutput, calls=%fused_computation.223 | convolution fusion | flops 4904188416 | bytes 24391680 | tf_op jit(solution)/shard_map/sqid,fd->sqif/dot_general | solution.py:280
  846.2 43.5 %reduce-scatter.16.cloned.1.call-done = bf16[2,2,256,768]{3,2,0,1:T(8,128)(2,1)} async-done(((bf16[2,2,512,768]{3,2,0,1:T(8,128)(2,1)}), bf16[2,2,256,768]{3,2,0,1:T(8,128)(2,1)}) %reduce-scatter.16.cloned.1.call-update) | async-done | bytes 1572880 | tf_op jit(solution)/shard_map/reduce_scatter | solution.py:288
  899.7 44.9 %all-gather.22.cloned.1.call-done = bf16[2,2,512,768]{3,2,0,1:T(8,128)(2,1)} async-done(((bf16[2,2,256,768]{3,2,0,1:T(8,128)(2,1)}), bf16[2,2,512,768]{3,2,0,1:T(8,128)(2,1)}) %all-gather.22.cloned.1.call-update) | async-done | bytes 3145744 | tf_op jit(solution)/shard_map/all_gather | solution.py:293
  950.7 267.6 %while.59 = (s32[]{:T(128)}, bf16[2,2,512,384]{2,3,0,1:T(8,128)(2,1)}, bf16[2,896,384]{1,2,0:T(8,128)(2,1)}, bf16[2,896,384]{1,2,0:T(8,128)(2,1)}, f32[2,6,64]{2...) while((s32[]{:T(128)}, ...), condition=%wide.region_43.44_spmd.clone, body=%wide.region_32.43_spmd.clone.sunk | while | flops 4063501824 | bytes 403456640 | solution.py:345
  993.7 15.7 multiply_reduce_fusion.10
  1009.3 11.5 multiply_reduce_fusion.11
  1020.8 17.7 %select_reduce_fusion.6 = (f32[6,512]{1,0:T(8,128)S(1)}, f32[6,512]{1,0:T(8,128)S(1)}, f32[6,896]{1,0:T(8,128)S(1)}, f32[6,896]{1,0:T(8,128)S(1)}, f32[6,512]{1,...) fusion(pred[512,896]{1,0:T(8,128)(4,1)S(1)} %dynamic-slice_bitc, ...), kind=kLoop, calls=%fused_computation.111.clone.1 | loop fusion | flops 55027200 | bytes 55625728 | tf_op jit(solution)/shard_map/while/body/eval_jaxpr/reduce_sum | solution.py:131
  1048.4 16.1 %fusion.550 = f32[6,32]{1,0:T(8,128)S(1)} fusion(s32[512,896]{1,0:T(8,128)S(1)} %copy-done.20, bf16[6,512,896]{2,1,0:T(8,128)(2,1)S(1)} %get-tuple-element.1080), kind=kOutput, calls=%fused_computation.157.clone.1 | convolution fusion | flops 190840832 | bytes 7340800 | tf_op jit(solution)/shard_map/while/body/eval_jaxpr/hij,rij->hr/dot_general | solution.py:139
  1064.5 15.9 %fusion.551 = f32[2,6,32]{2,1,0:T(8,128)S(1)} fusion(f32[2,6,32]{2,1,0:T(8,128)S(1)} %get-tuple-element.1221, s32[]{:T(128)S(6)} %copy.448, f32[6,32]{1,0:T(8,128)S(1)} %fusion.550, s32[512,896]{1,0:T(8,128)S(1)} %copy-done.20, bf16[6,512,896]{2,1,0:T(8,128)(2,1)S(1)} %get-tuple-element.1077), kind=kOutput, calls=%fused_computation.162.clone.1 | convolution fusion | flops 190841216 | bytes 7348228 | tf_op jit(solution)/shard_map/while/body/eval_jaxpr/hij,rij->hr/dot_general | solution.py:139
  1113.0 15.7 multiply_reduce_fusion.10
  1128.7 11.5 multiply_reduce_fusion.11
  1140.1 17.7 %select_reduce_fusion.6 = (f32[6,512]{1,0:T(8,128)S(1)}, f32[6,512]{1,0:T(8,128)S(1)}, f32[6,896]{1,0:T(8,128)S(1)}, f32[6,896]{1,0:T(8,128)S(1)}, f32[6,512]{1,...) fusion(pred[512,896]{1,0:T(8,128)(4,1)S(1)} %dynamic-slice_bitc, ...), kind=kLoop, calls=%fused_computation.111.clone.1 | loop fusion | flops 55027200 | bytes 55625728 | tf_op jit(solution)/shard_map/while/body/eval_jaxpr/reduce_sum | solution.py:131
  1167.7 16.1 %fusion.550 = f32[6,32]{1,0:T(8,128)S(1)} fusion(s32[512,896]{1,0:T(8,128)S(1)} %copy-done.20, bf16[6,512,896]{2,1,0:T(8,128)(2,1)S(1)} %get-tuple-element.1080), kind=kOutput, calls=%fused_computation.157.clone.1 | convolution fusion | flops 190840832 | bytes 7340800 | tf_op jit(solution)/shard_map/while/body/eval_jaxpr/hij,rij->hr/dot_general | solution.py:139
  1183.8 15.9 %fusion.551 = f32[2,6,32]{2,1,0:T(8,128)S(1)} fusion(f32[2,6,32]{2,1,0:T(8,128)S(1)} %get-tuple-element.1221, s32[]{:T(128)S(6)} %copy.448, f32[6,32]{1,0:T(8,128)S(1)} %fusion.550, s32[512,896]{1,0:T(8,128)S(1)} %copy-done.20, bf16[6,512,896]{2,1,0:T(8,128)(2,1)S(1)} %get-tuple-element.1077), kind=kOutput, calls=%fused_computation.162.clone.1 | convolution fusion | flops 190841216 | bytes 7348228 | tf_op jit(solution)/shard_map/while/body/eval_jaxpr/hij,rij->hr/dot_general | solution.py:139
  1231.0 9.6 fusion.153
  1243.6 10.0 fusion.150
  1266.8 39.9 %all-reduce = (f32[768]{0:T(1024)}, f32[768]{0:T(1024)}, f32[768]{0:T(1024)}, f32[768]{0:T(1024)}, f32[768]{0:T(1024)}) all-reduce(f32[768]{0:T(1024)S(1)} %copy-done.76, f32[768]{0:T(1024)S(1)} %copy-done.77, f32[768]{0:T(1024)S(1)} %copy-done.75, f32[768]{0:T(1024)S(1)} %copy-done.73, ...), channel_id=1, replica_groups=mesh['dp'=16,'tensor'=2] {'dp','tensor'}, use_global_device_ids=true, to_apply=%region_59.60 | all-reduce | flops 3840 | bytes 30720 | tf_op jit(solution)/shard_map/psum | solution.py:390
  1306.8 63.4 %all-reduce.1 = (f32[6,64]{1,0:T(8,128)}, f32[6,64]{1,0:T(8,128)}, f32[2,6,64]{2,0,1:T(2,128)}, f32[6,32]{1,0:T(8,128)}, f32[1536]{0:T(1024)}) all-reduce(f32[6,64]{1,0:T(8,128)S(1)} %reduce_sum.386, f32[6,64]{1,0:T(8,128)S(1)} %reduce_sum.387, f32[2,6,64]{2,0,1:T(2,128)S(1)} %reduce_sum.388, ...), channel_id=1, replica_groups=mesh['dp'=16,'tensor'=2] {'dp'}, use_global_device_ids=true, to_apply=%region_51.52 | all-reduce | flops 3264 | bytes 26112 | tf_op jit(solution)/shard_map/psum | solution.py:406
  1374.3 189.5 %all-reduce.5.cloned.1.call-done = (f32[768,384]{1,0:T(8,128)}, f32[768,384]{1,0:T(8,128)}, f32[768,384]{1,0:T(8,128)}, f32[384,768]{1,0:T(8,128)}, f32[768,1536]{1,0:T(8,128)}, /*index=5*/f32[1536,768]{1,0:T(8,128)}) async-done(((f32[768,384]{1,0:T(8,128)}, f32[768,384]{1,0:T(8,128)}, f32[768,384]{1,0:T(8,128)}, f32[384,768]{1,0:T(8,128)}, f32[768,1536]{1,0:T(8,128)}, /*index=5*/f32[1536,768]{1,0:T(8,128)}), ...) | async-done | bytes 14155792 | tf_op jit(solution)/shard_map/psum | solution.py:406
  (542 shorter events, 390.1 us)
Async XLA Ops:
  7.2 366.3 %copy-start = (bf16[768,1536]{1,0:T(8,128)(2,1)S(1)}, bf16[768,1536]{1,0:T(8,128)(2,1)}, u32[]{:S(2)}) copy-start(bf16[768,1536]{1,0:T(8,128)(2,1)} %param.49) | copy-start | bytes 7077892
  7.2 5.2 copy-start.81
  7.2 5.2 copy-start.72
  7.2 87.6 %all-gather.10.cloned.1.call-start = ((), (), s32[]{:S(2)}) async-start(), calls=%async_computation.7 | async-start | bytes 4718592 | tf_op jit(solution)/shard_map/all_gather | solution.py:200
  10.2 87.3 %all-gather.24.cloned.1.call-start = ((), (), s32[]{:S(2)}) async-start(), calls=%async_computation.21 | async-start | bytes 1769472 | tf_op jit(solution)/shard_map/all_gather | solution.py:201
  10.9 312.1 %reduce-scatter.8.cloned.1.call-start = ((), (), s32[]{:S(2)}) async-start(), calls=%async_computation.8 | async-start | bytes 4718592 | tf_op jit(solution)/shard_map/reduce_scatter | solution.py:237
  18.1 68.7 %copy-start.79 = (s32[1,2,512]{2,1,0:T(2,128)S(1)}, s32[1,2,512]{2,1,0:T(2,128)}, u32[]{:S(2)}) copy-start(s32[1,2,512]{2,1,0:T(2,128)} %param.59) | copy-start | bytes 12292
  109.3 13.6 copy-start.8
  122.9 5.3 copy-start.28
  176.9 13.4 copy-start.9
  190.3 13.5 copy-start.8
  203.8 5.3 copy-start.28
  257.8 13.4 copy-start.9
  276.6 50.0 %copy-start.61 = (f32[768]{0:T(1024)S(1)}, f32[768]{0:T(1024)}, u32[]{:S(2)}) copy-start(f32[768]{0:T(1024)} %param.47) | copy-start | bytes 9220
  276.7 50.0 %copy-start.63 = (f32[768]{0:T(1024)S(1)}, f32[768]{0:T(1024)}, u32[]{:S(2)}) copy-start(f32[768]{0:T(1024)} %param.48) | copy-start | bytes 9220
  276.7 96.8 %all-gather.12.cloned.1.call-start = ((), (), s32[]{:S(2)}) async-start(), calls=%async_computation.9 | async-start | bytes 4718592 | tf_op jit(solution)/shard_map/all_gather | solution.py:242
  326.6 46.9 %copy-start.89 = (f32[1536]{0:T(1024)S(1)}, f32[1536]{0:T(1024)}, u32[]{:S(2)}) copy-start(f32[1536]{0:T(1024)} %param.50) | copy-start | bytes 18436
  328.4 104.8 %reduce-scatter.10.cloned.1.call-start = ((), (), s32[]{:S(2)}) async-start(), calls=%async_computation.10 | async-start | bytes 4718592 | tf_op jit(solution)/shard_map/reduce_scatter | solution.py:246
  373.5 9.7 copy-start.84
  389.6 43.6 %copy-start.66 = (f32[768]{0:T(1024)S(1)}, f32[768]{0:T(1024)}, u32[]{:S(2)}) copy-start(f32[768]{0:T(1024)} %param.52) | copy-start | bytes 9220
  389.6 98.2 %all-gather.16.cloned.1.call-start = ((), (), s32[]{:S(2)}) async-start(), calls=%async_computation.12 | async-start | bytes 4718592 | tf_op jit(solution)/shard_map/all_gather | solution.py:200
  442.8 69.4 %all-gather.14.cloned.1.call-start = ((), (), s32[]{:S(2)}) async-start(), calls=%async_computation.11 | async-start | bytes 1769472 | tf_op jit(solution)/shard_map/all_gather | solution.py:201
  443.5 203.7 %reduce-scatter.12.cloned.1.call-start = ((), (), s32[]{:S(2)}) async-start(), calls=%async_computation.13 | async-start | bytes 4718592 | tf_op jit(solution)/shard_map/reduce_scatter | solution.py:237
  603.7 47.2 %copy-start.62 = (f32[768]{0:T(1024)S(1)}, f32[768]{0:T(1024)}, u32[]{:S(2)}) copy-start(f32[768]{0:T(1024)} %param.47) | copy-start | bytes 9220
  603.7 47.2 %copy-start.64 = (f32[768]{0:T(1024)S(1)}, f32[768]{0:T(1024)}, u32[]{:S(2)}) copy-start(f32[768]{0:T(1024)} %param.48) | copy-start | bytes 9220
  603.7 94.2 %all-gather.18.cloned.1.call-start = ((), (), s32[]{:S(2)}) async-start(), calls=%async_computation.14 | async-start | bytes 4718592 | tf_op jit(solution)/shard_map/all_gather | solution.py:242
  650.9 47.1 %copy-start.90 = (f32[1536]{0:T(1024)S(1)}, f32[1536]{0:T(1024)}, u32[]{:S(2)}) copy-start(f32[1536]{0:T(1024)} %param.50) | copy-start | bytes 18436
  652.9 110.0 %reduce-scatter.14.cloned.1.call-start = ((), (), s32[]{:S(2)}) async-start(), calls=%async_computation.15 | async-start | bytes 4718592 | tf_op jit(solution)/shard_map/reduce_scatter | solution.py:246
  697.9 15.0 copy-start.85
  719.3 43.6 %copy-start.67 = (f32[768]{0:T(1024)S(1)}, f32[768]{0:T(1024)}, u32[]{:S(2)}) copy-start(f32[768]{0:T(1024)} %param.52) | copy-start | bytes 9220
  719.3 101.1 %all-gather.20.cloned.1.call-start = ((), (), s32[]{:S(2)}) async-start(), calls=%async_computation.16 | async-start | bytes 4718592 | tf_op jit(solution)/shard_map/all_gather | solution.py:276
  775.3 114.5 %reduce-scatter.16.cloned.1.call-start = ((), (), s32[]{:S(2)}) async-start(), calls=%async_computation.17 | async-start | bytes 4718592 | tf_op jit(solution)/shard_map/reduce_scatter | solution.py:288
  846.2 43.6 %copy-start.7 = (bf16[2,2,256,768]{3,2,0,1:T(8,128)(2,1)S(1)}, bf16[2,2,256,768]{3,2,0,1:T(8,128)(2,1)}, u32[]{:S(2)}) copy-start(bf16[2,2,256,768]{3,2,0,1:T(8,128)(2,1)} %pad_maximum_fusion.15) | copy-start | bytes 4718596
  846.2 98.4 %all-gather.22.cloned.1.call-start = ((), (), s32[]{:S(2)}) async-start(), calls=%async_computation.18 | async-start | bytes 4718592 | tf_op jit(solution)/shard_map/all_gather | solution.py:293
  898.2 46.5 %copy-start.88 = (bf16[384,768]{1,0:T(8,128)(2,1)S(1)}, bf16[384,768]{1,0:T(8,128)(2,1)}, u32[]{:S(2)}) copy-start(bf16[384,768]{1,0:T(8,128)(2,1)} %param.42) | copy-start | bytes 1769476
  899.6 470.7 %reduce-scatter.18.cloned.1.call-start = ((), (), s32[]{:S(2)}) async-start(), calls=%async_computation.19 | async-start | bytes 4718592 | tf_op jit(solution)/shard_map/reduce_scatter | solution.py:382
  979.8 4.8 copy-start.5
  987.5 21.8 %copy-start.3 = (f32[6,512,896]{2,1,0:T(8,128)}, f32[6,512,896]{2,1,0:T(8,128)S(1)}, u32[]{:S(2)}) copy-start(f32[6,512,896]{2,1,0:T(8,128)S(1)} %fusion.531) | copy-start | bytes 33030148 | tf_op jit(solution)/shard_map/while
  1038.6 7.3 copy-start.2
  1106.8 21.8 %copy-start.3 = (f32[6,512,896]{2,1,0:T(8,128)}, f32[6,512,896]{2,1,0:T(8,128)S(1)}, u32[]{:S(2)}) copy-start(f32[6,512,896]{2,1,0:T(8,128)S(1)} %fusion.531) | copy-start | bytes 33030148 | tf_op jit(solution)/shard_map/while
  1157.9 7.3 copy-start.2
  1231.0 143.4 %reduce-scatter.20.cloned.1.call-start = ((), (), s32[]{:S(2)}) async-start(), calls=%async_computation.20 | async-start | bytes 1769472 | tf_op jit(solution)/shard_map/reduce_scatter | solution.py:385
  1243.5 320.4 %all-reduce.5.cloned.1.call-start = ((), (), s32[]{:S(2)}) async-start(), calls=%async_computation.22 | async-start | bytes 28311552 | tf_op jit(solution)/shard_map/psum | solution.py:406
  1243.5 10.0 copy-start.39
  1243.5 10.0 copy-start.50
  1243.5 10.0 copy-start.86
  1265.6 41.3 %copy-start.78 = (f32[1536]{0:T(1024)S(1)}, f32[1536]{0:T(1024)}, u32[]{:S(2)}) copy-start(f32[1536]{0:T(1024)} %get-tuple-element.679) | copy-start | bytes 18436
  1265.6 104.7 %copy-start.71 = (f32[2,2,256]{2,0,1:T(2,128)S(1)}, f32[2,2,256]{2,0,1:T(2,128)}, u32[]{:S(2)}) copy-start(f32[2,2,256]{2,0,1:T(2,128)} %copy-done.70) | copy-start | bytes 12292
  (85 other events, 236.8 us)
Sparse Core Ops, SparseCore 0:
  10.3 47.6 all-gather.9
  59.5 22.7 all-gather.23
  276.8 46.2 reduce-scatter.7
  328.5 44.8 all-gather.11
  389.7 43.4 reduce-scatter.9
  442.9 44.8 all-gather.15
  489.4 22.7 all-gather.13
  603.8 43.4 reduce-scatter.11
  653.0 44.8 all-gather.17
  719.4 43.4 reduce-scatter.13
  775.4 44.8 all-gather.19
  846.3 43.4 reduce-scatter.15
  899.7 44.8 all-gather.21
  1231.1 43.4 reduce-scatter.17
  1277.8 22.2 reduce-scatter.19
  1306.8 257.0 all-reduce.4
where the time goes:
time: 1590 us; the launch traced here: 1580 us
  waiting for transfers between devices  657 us (41%)
  matrix products  482 us (30%)
  other arithmetic  149 us (9%)
  local copies, waits for them, and re-layouts  143 us (9%)
  blocking collectives  103 us (6%)
  loops' own time  31.2 us (2%)
    psum x1, waiting for transfers between devices, per_device(): lax.psum((weight_terms[0], weight_terms[1], weight_terms[2], weight_terms...  190 us
    dot_general x12, matrix products, score_block(): jnp.einsum('ihd,jhd->hij', queries, key_rows, preferred_element_type=jnp....  121 us
    all_gather x2, waiting for transfers between devices, forward_pass(): lax.all_gather(normed.astype(jnp.bfloat16), 'tensor', axis=2, tiled=True)  90 us
    reduce_scatter x2, waiting for transfers between devices, forward_pass(): lax.psum_scatter(projected.astype(jnp.bfloat16), 'tensor', scatter_dimens...  89.8 us
    reduce_scatter x2, waiting for transfers between devices, forward_pass(): lax.psum_scatter(ffn_part.astype(jnp.bfloat16), 'tensor', scatter_dimensi...  87.1 us
    dot_general x4, matrix products, attend_backward(): jnp.einsum('hij,rij->hr', d_scores, one_hot, preferred_element_type=jnp.f...  64 us
    psum x1, blocking collectives, per_device(): lax.psum((weight_terms[0], weight_terms[1], weight_terms[2], weight_terms...  63.4 us
    dot_general x8, matrix products, attend_forward(): jnp.einsum('hij,jhd->ihd', weights, value_rows, preferred_element_type=jn...  58.4 us
  transfers between devices with their start and end apart: 16, of which 12 were waited for; matrix products, arithmetic and copies ran while one was open for 8% of the time, Pallas kernels for 0%

commit v1 on v0

v1 whole, which is shorter than its diff:
```python
import jax
import jax.numpy as jnp
from jax import lax
from jax.experimental import pallas as pl
from jax.experimental.pallas import tpu as pltpu
from jax.sharding import PartitionSpec as P

HDIM = 64
NREL = 32
epsilon = 1e-05
masked_score = -1e30
target_floor = 48
distance_steps = (1, 2, 3, 4, 5, 6, 7, 8, 12, 16, 24, 32, 64, 128, 256)
highest = lax.Precision.HIGHEST
f32 = jnp.float32
bf16 = jnp.bfloat16
LANES = 128
ORDERS = 16
SCALE = HDIM ** (-0.5)


def bucket_of(distance):
    magnitude = jnp.abs(distance)
    counted = jnp.zeros(distance.shape, jnp.int32)
    for threshold in distance_steps:
        counted = counted + (magnitude >= threshold).astype(jnp.int32)
    return counted + NREL // 2 * (distance > 0).astype(jnp.int32)


def diagonal_buckets(half, rows, mem_rows):
    pieces = []
    for width, off in (
        (rows, 0),
        (rows, jnp.where(half == 0, -rows, rows)),
        (mem_rows, rows * half + mem_rows),
    ):
        length = width + rows
        lane = jnp.arange(length, dtype=jnp.int32)
        pieces.append(off + jnp.where(lane < width, -lane, length - lane))
    return bucket_of(jnp.concatenate(pieces))


def mask_lanes(bucket, doc_len, perm_rank, seg_ids, mem_seg):
    slot_rows = perm_rank.shape[0]
    mem_rows = mem_seg.shape[0]
    docs = doc_len.shape[0]
    positions = jnp.arange(slot_rows, dtype=jnp.int32)
    document = positions // bucket
    within = positions - document * bucket
    doc_index = jnp.arange(docs, dtype=jnp.int32)
    doc_length = jnp.sum(
        jnp.where(document[:, None] == doc_index[None, :], doc_len[None, :], 0), axis=1, dtype=jnp.int32
    )
    absent = within >= doc_length
    order = jnp.where(within < 2, 0, jnp.maximum(perm_rank - target_floor, 0))
    lane = jnp.arange(HDIM, dtype=jnp.int32)[None, :]
    slot_order = lane - 6
    slot_doc = lane - 6 - ORDERS
    in_order = (slot_order >= 0) & (slot_order < ORDERS)
    in_doc = (slot_doc >= 0) & (slot_doc < docs)
    is_absent = lane == 6 + ORDERS + docs
    one = (lane == 4) | (lane == 5)
    hide_doc = in_doc & (slot_doc != document[:, None])
    hide_content = in_order & (slot_order > order[:, None])
    hide_query = in_order & (slot_order >= order[:, None]) & (slot_order > 0)

    def query_side(hide):
        return jnp.where(one, 1.0, jnp.where(hide | hide_doc | is_absent, masked_score, 0.0))

    query_lanes = jnp.stack([query_side(hide_content), query_side(hide_query)])
    seg_lane = (lane == 2) | (lane == 3)
    ones_lane = lane < 2

    def key_side(segment, extra):
        return jnp.where(ones_lane, 1.0, jnp.where(seg_lane, segment[:, None].astype(f32), extra))

    token_hot = (
        (in_order & (slot_order == order[:, None]))
        | (in_doc & (slot_doc == document[:, None]))
        | (is_absent & absent[:, None])
    )
    key_lanes = key_side(seg_ids, token_hot.astype(f32))
    mem_lanes = key_side(mem_seg, jnp.zeros((mem_rows, HDIM), f32))

    def both(values_in):
        return jnp.concatenate([values_in, values_in], axis=-1).astype(bf16)

    return both(query_lanes), both(key_lanes), both(mem_lanes)


def split_pair(values_in):
    high = values_in.astype(bf16)
    return high, (values_in - high.astype(f32)).astype(bf16)


def head_tables(content_bias, seg_bias, seg_embed):
    heads = content_bias.shape[0]
    parity = (jnp.arange(heads) % 2)[:, None, None]
    row = jnp.arange(LANES)[None, :, None]
    lane = jnp.arange(LANES)[None, None, :]
    own_row = (row // HDIM) == parity
    spare = (lane // HDIM) != parity
    column = lane % HDIM

    def spread(vectors, lanes):
        tall = jnp.concatenate([vectors, vectors], axis=1)[:, :, None]
        keep = own_row & spare & ((column == lanes[0]) | (column == lanes[1]))
        parts = split_pair(tall)
        return jnp.concatenate([jnp.where(keep, part, jnp.zeros((), bf16)) for part in parts], axis=1)

    first, second = seg_embed[0], seg_embed[1]
    same_seg_one = spread(first, (0, 1)) + spread(second - first, (2, 3))
    same_seg_zero = spread(second, (0, 1)) + spread(first - second, (2, 3))
    seg_table = jnp.concatenate([same_seg_one, same_seg_zero], axis=2)
    key_table = spread(content_bias * SCALE, (4, 5))
    dots = [jnp.sum(seg_bias * part, axis=-1)[:, None] * SCALE for part in (first, second)]
    column = column[:, 0]
    spare = spare[:, 0]

    def const_row(start, slope):
        return jnp.where(spare & (column < 2), start, jnp.where(spare & (column >= 2) & (column < 4), slope, 0.0))

    seg_const = jnp.stack(
        [const_row(dots[0], dots[1] - dots[0]), const_row(dots[1], dots[0] - dots[1])], axis=1
    )
    return seg_table, seg_const, key_table


def nt(left, right):
    return lax.dot_general(left, right, (((1,), (1,)), ((), ())), preferred_element_type=f32)


def nn(left, right):
    return lax.dot_general(left, right, (((1,), (0,)), ((), ())), preferred_element_type=f32)


def tn(left, right):
    return lax.dot_general(left, right, (((0,), (0,)), ((), ())), preferred_element_type=f32)


def lane_of(shape):
    return lax.broadcasted_iota(jnp.int32, shape, len(shape) - 1)


def high_low(values_in, lane):
    high = values_in.astype(bf16).astype(f32)
    return jnp.where(lane % 2 == 0, high, values_in - high)


def attend_kernel(
    full_ref, q_ref, ko_ref, vo_ref, ke_ref, ve_ref, qm_ref, kmo_ref, kme_ref, seg_ref,
    st_ref, sc_ref, kt_ref, diag_ref,
    a_ref, po_ref, pe_ref,
    bo_ref, be_ref,
):
    slot = pl.program_id(1)
    rows = q_ref.shape[2]
    mem_rows = ke_ref.shape[1] - rows

    @pl.when(slot == 0)
    def _():
        for head in range(2):
            start = 0
            for ref, at, width in ((bo_ref, 0, rows), (be_ref, 0, rows), (be_ref, rows, mem_rows)):
                length = width + rows
                line = jnp.broadcast_to(diag_ref[head, :, start : start + length], (rows, length))
                skew = pltpu.roll(line, 0, 1, stride=1, stride_axis=0)
                ref[head, :, at : at + width] = skew[:, :width] * SCALE
                start += length

    lane = lane_of((rows, LANES))
    eye = lax.broadcasted_iota(jnp.int32, (rows, rows), 0) == lax.broadcasted_iota(jnp.int32, (rows, rows), 1)

    def keys_of(k_ref, km_ref, head):
        key_rows = k_ref[0]
        key_lane = lane_of(key_rows.shape)
        shift = nn(jnp.concatenate([key_rows, key_rows], axis=1), kt_ref[head])
        spare = high_low(shift, key_lane) + km_ref[0].astype(f32)
        return jnp.where(key_lane // HDIM == head, key_rows.astype(f32), spare).astype(bf16)

    def run(full):
        keys = [
            (keys_of(ko_ref, kmo_ref, head), keys_of(ke_ref, kme_ref, head) if full else None)
            for head in range(2)
        ]
        for stream in range(2):
            outs = []
            for head in range(2):
                own = lane // HDIM == head
                scaled = q_ref[0, stream] * jnp.asarray(SCALE, bf16)
                table = nn(jnp.concatenate([scaled, scaled], axis=1), st_ref[head])
                seg = jnp.where(
                    seg_ref[0] > 0,
                    table[:, :LANES] + sc_ref[head, 0:1],
                    table[:, LANES:] + sc_ref[head, 1:2],
                )
                spare = high_low(seg, lane) + qm_ref[0, stream].astype(f32)
                queries = jnp.where(own, scaled.astype(f32), spare).astype(bf16)
                key_own, key_ext = keys[head]
                score_own = nt(queries, key_own)
                if stream == 0:
                    plain = own | (lane % HDIM < 6)
                    product = jnp.where(plain, queries.astype(f32) * key_own.astype(f32), 0.0)
                    self_score = jnp.sum(product, axis=1, keepdims=True)
                else:
                    self_score = masked_score
                score_own = jnp.where(eye, self_score, score_own) + bo_ref[head]
                top = jnp.max(score_own, axis=1, keepdims=True)
                if full:
                    score_ext = nt(queries, key_ext) + be_ref[head]
                    top = jnp.maximum(top, jnp.max(score_ext, axis=1, keepdims=True))
                part_own = jnp.exp(score_own - top)
                total = jnp.sum(part_own, axis=1, keepdims=True)
                if full:
                    part_ext = jnp.exp(score_ext - top)
                    total = total + jnp.sum(part_ext, axis=1, keepdims=True)
                inverse = 1.0 / total
                weight_own = (part_own * inverse).astype(bf16)
                po_ref[0, stream, head] = weight_own
                out = nn(weight_own, vo_ref[0])
                if full:
                    weight_ext = (part_ext * inverse).astype(bf16)
                    pe_ref[0, stream, head] = weight_ext
                    out = out + nn(weight_ext, ve_ref[0])
                outs.append(out)
            a_ref[0, stream] = jnp.where(lane < HDIM, outs[0], outs[1]).astype(bf16)

    is_full = full_ref[slot] > 0

    @pl.when(is_full)
    def _():
        run(True)

    @pl.when(jnp.logical_not(is_full))
    def _():
        run(False)


def specs_of(rows, ext):
    by_pair = pl.BlockSpec((1, 2, rows, LANES), lambda p, s, *_: (s, 0, 0, p))
    own = pl.BlockSpec((1, rows, LANES), lambda p, s, *_: (s, 0, p))
    far = pl.BlockSpec((1, ext, LANES), lambda p, s, *_: (s, 0, p))
    own_lanes = pl.BlockSpec((1, rows, LANES), lambda p, s, *_: (s, 0, 0))
    far_lanes = pl.BlockSpec((1, ext, LANES), lambda p, s, *_: (s, 0, 0))
    query_lanes = pl.BlockSpec((1, 2, rows, LANES), lambda p, s, *_: (s, 0, 0, 0))
    weight_own = pl.BlockSpec((1, 2, 2, rows, rows), lambda p, s, *_: (s, 0, p, 0, 0))
    weight_far = pl.BlockSpec((1, 2, 2, rows, ext), lambda p, s, *_: (s, 0, p, 0, 0))
    return by_pair, own, far, own_lanes, far_lanes, query_lanes, weight_own, weight_far


def per_head(*shape):
    return pl.BlockSpec((2,) + shape, lambda p, s, *_: (p,) + (0,) * len(shape))


def attend(full, queries, key_own, value_own, key_ext, value_ext, lanes, tables, diagonals):
    slots, streams, rows, width = queries.shape
    ext = key_ext.shape[1]
    heads = width // HDIM
    query_lanes, own_lanes, ext_lanes, seg_rows = lanes
    seg_table, seg_const, key_table = tables
    pair, own, far, own_l, far_l, query_l, w_own, w_far = specs_of(rows, ext)
    return pl.pallas_call(
        attend_kernel,
        grid_spec=pltpu.PrefetchScalarGridSpec(
            num_scalar_prefetch=1,
            grid=(heads // 2, slots),
            in_specs=[
                pair, own, own, far, far, query_l, own_l, far_l, own_l,
                per_head(2 * LANES, 2 * LANES), per_head(2, LANES), per_head(2 * LANES, LANES),
                per_head(1, diagonals.shape[-1]),
            ],
            out_specs=[pair, w_own, w_far],
            scratch_shapes=[pltpu.VMEM((2, rows, rows), f32), pltpu.VMEM((2, rows, ext), f32)],
        ),
        out_shape=[
            jax.ShapeDtypeStruct(queries.shape, bf16),
            jax.ShapeDtypeStruct((slots, streams, heads, rows, rows), bf16),
            jax.ShapeDtypeStruct((slots, streams, heads, rows, ext), bf16),
        ],
        name="attend",
    )(full, queries, key_own, value_own, key_ext, value_ext, query_lanes, own_lanes, ext_lanes, seg_rows,
      seg_table, seg_const, key_table, diagonals)


def attend_back_kernel(
    full_ref, q_ref, ko_ref, vo_ref, ke_ref, ve_ref, kmo_ref, kme_ref, seg_ref,
    a_ref, da_ref, po_ref, pe_ref, emb_ref, cb_ref,
    dq_ref, dko_ref, dvo_ref, dke_ref, dve_ref, small_ref, diag_ref,
    bo_ref, be_ref,
):
    slot = pl.program_id(1)
    rows = q_ref.shape[2]
    ext = ke_ref.shape[1]
    lane = lane_of((rows, LANES))

    @pl.when(slot == 0)
    def _():
        bo_ref[...] = jnp.zeros_like(bo_ref)
        be_ref[...] = jnp.zeros_like(be_ref)
        small_ref[...] = jnp.zeros_like(small_ref)

    def keys_of(k_ref, km_ref, head):
        key_lane = lane_of(k_ref.shape[1:])
        return jnp.where(key_lane // HDIM == head, k_ref[0], km_ref[0])

    def run(full):
        parts = [(ko_ref, vo_ref, kmo_ref, po_ref, bo_ref, dko_ref, dvo_ref)]
        if full:
            parts.append((ke_ref, ve_ref, kme_ref, pe_ref, be_ref, dke_ref, dve_ref))
        d_queries = [[None, None], [None, None]]
        for head in range(2):
            own = lane // HDIM == head
            base = HDIM * (1 - head)
            key_sets = [keys_of(k_ref, km_ref, head) for k_ref, _, km_ref, *_ in parts]
            d_keys = [0.0] * len(parts)
            d_values = [0.0] * len(parts)
            totals = [jnp.zeros((1, LANES), f32)] * 5
            for stream in range(2):
                queries = q_ref[0, stream]
                flat = jnp.where(
                    own,
                    queries.astype(f32) * SCALE,
                    jnp.where(lane % HDIM == 4, 1.0, 0.0),
                ).astype(bf16)
                cot = jnp.where(own, da_ref[0, stream].astype(f32), 0.0)
                inner = jnp.sum(cot * a_ref[0, stream].astype(f32), axis=1, keepdims=True)
                cot = cot.astype(bf16)
                d_rows = 0.0
                for at, (k_ref, v_ref, km_ref, p_ref, b_ref, dk_ref, dv_ref) in enumerate(parts):
                    weights = p_ref[0, stream, head]
                    d_scores = weights.astype(f32) * (nt(cot, v_ref[0]) - inner)
                    b_ref[head] += d_scores
                    d_scores = d_scores.astype(bf16)
                    d_rows = d_rows + nn(d_scores, key_sets[at])
                    d_keys[at] = d_keys[at] + tn(flat, d_scores)
                    d_values[at] = d_values[at] + tn(cot, weights)
                every = d_rows[:, base : base + 1]
                ones = d_rows[:, base + 2 : base + 3]
                same = jnp.where(seg_ref[0] > 0, ones, every - ones)
                other = every - same
                d_queries[stream][head] = SCALE * (
                    d_rows + other * emb_ref[head, 0:1] + same * emb_ref[head, 1:2]
                )
                wide = queries.astype(f32)
                for row, member in enumerate((other * wide, same * wide, other, same, d_rows)):
                    totals[row] = totals[row] + jnp.sum(member, axis=0, keepdims=True)
            for row in range(5):
                small_ref[head, row : row + 1] += totals[row]
            for at, (k_ref, v_ref, km_ref, p_ref, b_ref, dk_ref, dv_ref) in enumerate(parts):
                column = d_keys[at][base + 4 : base + 5]
                mine = slice(HDIM * head, HDIM * head + HDIM)
                dk_ref[0, mine] = (d_keys[at][mine] + cb_ref[head] * SCALE * column).astype(bf16)
                dv_ref[0, mine] = d_values[at][mine].astype(bf16)
        for stream in range(2):
            dq_ref[0, stream] = jnp.where(lane < HDIM, d_queries[stream][0], d_queries[stream][1]).astype(bf16)

    is_full = full_ref[slot] > 0

    @pl.when(is_full)
    def _():
        run(True)

    @pl.when(jnp.logical_not(is_full))
    def _():
        run(False)
        dke_ref[...] = jnp.zeros_like(dke_ref)
        dve_ref[...] = jnp.zeros_like(dve_ref)

    @pl.when(slot == pl.num_programs(1) - 1)
    def _():
        for head in range(2):
            start = 0
            for ref, at, width in ((bo_ref, 0, rows), (be_ref, 0, rows), (be_ref, rows, ext - rows)):
                length = width + rows
                block = jnp.concatenate([ref[head, :, at : at + width], jnp.zeros((rows, rows), f32)], axis=1)
                step = rows // 2
                while step >= 8:
                    block = block[:step] + pltpu.roll(block[step:], length - step, 1)
                    step //= 2
                diag_ref[head, :, start : start + length] = block
                start += length


def attend_back(
    full, queries, key_own, value_own, key_ext, value_ext, lanes, attended, d_attended, weights,
    seg_rows_embed, bias_columns, diag_length,
):
    slots, streams, rows, width = queries.shape
    ext = key_ext.shape[1]
    heads = width // HDIM
    _, own_lanes, ext_lanes, seg_rows = lanes
    pair, own, far, own_l, far_l, query_l, w_own, w_far = specs_of(rows, ext)
    tall_own = pl.BlockSpec((1, LANES, rows), lambda p, s, *_: (s, p, 0))
    tall_ext = pl.BlockSpec((1, LANES, ext), lambda p, s, *_: (s, p, 0))
    return pl.pallas_call(
        attend_back_kernel,
        grid_spec=pltpu.PrefetchScalarGridSpec(
            num_scalar_prefetch=1,
            grid=(heads // 2, slots),
            in_specs=[
                pair, own, own, far, far, own_l, far_l, own_l, pair, pair, w_own, w_far,
                per_head(2, LANES), per_head(HDIM, 1),
            ],
            out_specs=[pair, tall_own, tall_own, tall_ext, tall_ext, per_head(8, LANES), per_head(8, diag_length)],
            scratch_shapes=[pltpu.VMEM((2, rows, rows), f32), pltpu.VMEM((2, rows, ext), f32)],
        ),
        out_shape=[
            jax.ShapeDtypeStruct(queries.shape, bf16),
            jax.ShapeDtypeStruct((slots, width, rows), bf16),
            jax.ShapeDtypeStruct((slots, width, rows), bf16),
            jax.ShapeDtypeStruct((slots, width, ext), bf16),
            jax.ShapeDtypeStruct((slots, width, ext), bf16),
            jax.ShapeDtypeStruct((heads, 8, LANES), f32),
            jax.ShapeDtypeStruct((heads, 8, diag_length), f32),
        ],
        name="attend_back",
    )(full, queries, key_own, value_own, key_ext, value_ext, own_lanes, ext_lanes, seg_rows,
      attended, d_attended, weights[0], weights[1], seg_rows_embed, bias_columns)


def other_of(values_in):
    size = lax.axis_size("tensor")
    return lax.ppermute(values_in, "tensor", [(i, (i + 1) % size) for i in range(size)])


def in_order(half, mine, other, axis):
    first = jnp.where(half == 0, mine, other)
    second = jnp.where(half == 0, other, mine)
    return jnp.concatenate([first, second], axis=axis)


def gather_rows(values_in):
    parts = lax.axis_size("dp")
    rows = values_in.shape[0] // parts
    piece = lax.dynamic_slice_in_dim(values_in, lax.axis_index("dp") * rows, rows, 0)
    whole = lax.all_gather(piece, ("tensor", "dp"), axis=0, tiled=True)
    return whole.reshape((lax.axis_size("tensor"),) + values_in.shape)


def sum_rows(parts):
    halves, rows, columns = parts.shape
    dp = lax.axis_size("dp")
    pad = -rows % (8 * dp)
    if pad:
        parts = jnp.pad(parts, ((0, 0), (0, pad), (0, 0)))
    flat = parts.astype(bf16).reshape(-1, columns)
    piece = lax.psum_scatter(flat, ("tensor", "dp"), scatter_dimension=0, tiled=True)
    return lax.all_gather(piece, "dp", axis=0, tiled=True)[:rows].astype(f32)


def norm_parts(values_in):
    centred = values_in - jnp.mean(values_in, axis=-1, keepdims=True)
    spread = jnp.mean(centred * centred, axis=-1, keepdims=True)
    return centred, lax.rsqrt(spread + epsilon)


def norm_back(cotangent, gain, centred, inverse):
    unit = centred * inverse
    scaled = cotangent * gain
    first = jnp.mean(scaled, axis=-1, keepdims=True)
    second = jnp.mean(scaled * unit, axis=-1, keepdims=True)
    return inverse * (scaled - first - unit * second), unit


def gelu_pair(values_in):
    rate = 0.7978845608028654
    square = values_in * values_in
    bent = jnp.tanh(rate * values_in * (1.0 + 0.044715 * square))
    half = 0.5 * (1.0 + bent)
    slope = half + 0.5 * values_in * (1.0 - bent * bent) * rate * (1.0 + 3 * 0.044715 * square)
    return values_in * half, slope


def dot_to(equation, left, right):
    return jnp.einsum(equation, left, right, preferred_element_type=f32)


def per_device(
    h_in, g_in, mem_in, d_h_out, d_g_out, w_query, w_key, w_value, w_out, content_bias, seg_bias,
    seg_embed, rel_table, norm1_gain, norm1_bias, w_in, b_in, w_ffo, b_ffo, norm2_gain, norm2_bias,
    bucket_len, doc_len, seg_ids, mem_seg, perm_rank,
):
    half = lax.axis_index("tensor")
    content, stream, memory = h_in[0], g_in[0], mem_in[0]
    slots, rows, width = content.shape
    mem_half = memory.shape[1]
    slot_rows = perm_rank.shape[2]
    mem_rows = mem_seg.shape[2]
    heads_half = w_query.shape[1] // HDIM

    other_rows = other_of(jnp.concatenate([content, memory], axis=1))
    table_half = jnp.concatenate(
        [content_bias, seg_bias, seg_embed[0], seg_embed[1], rel_table], axis=1
    )
    small_half = jnp.concatenate([table_half.reshape(-1), b_in])
    small_other = other_of(small_half)
    cut = table_half.size
    tables = in_order(half, table_half, small_other[:cut].reshape(table_half.shape), 0)
    hidden_bias = in_order(half, b_in, small_other[cut:], 0)
    content_all, seg_all = tables[:, :HDIM], tables[:, HDIM : 2 * HDIM]
    embed_all = jnp.stack([tables[:, 2 * HDIM : 3 * HDIM], tables[:, 3 * HDIM : 4 * HDIM]])
    rel_all = tables[:, 4 * HDIM :]
    heads = rel_all.shape[0]
    wq, wk, wv = gather_rows(w_query), gather_rows(w_key), gather_rows(w_value)
    w_out_all = gather_rows(w_out).reshape(-1, width)
    w_in_all = gather_rows(w_in)
    w_ffo_all = gather_rows(w_ffo).reshape(-1, width)

    full = (bucket_len[0] == slot_rows).astype(jnp.int32)
    query_lanes, key_lanes, mem_lanes = jax.vmap(mask_lanes)(
        bucket_len[0], doc_len[0], perm_rank[0], seg_ids[0], mem_seg[0]
    )
    start = half * rows
    far = slot_rows - rows - start

    def own_of(values_in, axis):
        return lax.dynamic_slice_in_dim(values_in, start, rows, axis)

    seg_rows = jnp.broadcast_to(
        own_of(seg_ids[0], 1).astype(f32)[:, :, None], (slots, rows, LANES)
    )
    lanes = (
        own_of(query_lanes, 2),
        own_of(key_lanes, 1),
        jnp.concatenate([lax.dynamic_slice_in_dim(key_lanes, far, rows, 1), mem_lanes], axis=1),
        seg_rows,
    )
    head_set = head_tables(content_all, seg_all, embed_all)
    buckets = diagonal_buckets(half, rows, mem_rows)
    hot = (buckets[None] == jnp.arange(NREL, dtype=jnp.int32)[:, None]).astype(f32)
    diagonals = jnp.dot(rel_all, hot, precision=highest)[:, None]

    pair = jnp.stack([content, stream], axis=1)

    def project(values_in, weight):
        out = dot_to("sjd,tde->sjte", values_in, weight)
        return out.reshape(values_in.shape[:-1] + (-1,)).astype(bf16)

    flat_pair = pair.reshape(slots, 2 * rows, width)
    queries = project(flat_pair, wq).reshape(slots, 2, rows, -1)
    ext_rows = jnp.concatenate(
        [other_rows[:, :rows], in_order(half, memory, other_rows[:, rows:], 1)], axis=1
    )
    key_own, value_own = project(content, wk), project(content, wv)
    key_ext, value_ext = project(ext_rows, wk), project(ext_rows, wv)

    attended, weight_own, weight_ext = attend(
        full, queries, key_own, value_own, key_ext, value_ext, lanes, head_set, diagonals
    )

    flat_rows = slots * 2 * rows
    attended_flat = attended.reshape(flat_rows, width)
    mid = pair.reshape(flat_rows, width).astype(f32) + dot_to("re,ed->rd", attended_flat, w_out_all)
    centred1, inverse1 = norm_parts(mid)
    normed = centred1 * inverse1 * norm1_gain + norm1_bias
    normed_low = normed.astype(bf16)
    ff_half = w_in.shape[1]
    hidden = dot_to("rd,tdf->rtf", normed_low, w_in_all).reshape(flat_rows, -1) + hidden_bias
    active, slope = gelu_pair(hidden)
    active = active.astype(bf16)
    second = normed + dot_to("rf,fd->rd", active, w_ffo_all) + b_ffo
    centred2, inverse2 = norm_parts(second)
    outputs = (centred2 * inverse2 * norm2_gain + norm2_bias).astype(bf16).reshape(pair.shape)

    cot = jnp.stack([d_h_out[0], d_g_out[0]], axis=1).reshape(flat_rows, width).astype(f32)
    d_second, unit2 = norm_back(cot, norm2_gain, centred2, inverse2)
    d_norm2_gain = jnp.sum(cot * unit2, axis=0)
    d_norm2_bias = jnp.sum(cot, axis=0)
    d_ffn = d_second.astype(bf16)
    d_b_ffo = jnp.sum(d_ffn.astype(f32), axis=0)
    d_w_ffo = dot_to("rf,rd->fd", active, d_ffn)
    d_hidden = (dot_to("rd,fd->rf", d_ffn, w_ffo_all) * slope).astype(bf16)
    d_b_in = jnp.sum(d_hidden.astype(f32), axis=0)
    d_w_in = dot_to("rf,rd->fd", d_hidden, normed_low)
    ffn_sums = sum_rows(
        jnp.concatenate(
            [member.astype(bf16).reshape(2, ff_half, width) for member in (d_w_ffo, d_w_in)], axis=1
        )
    )
    d_normed = d_second + dot_to("rtf,tdf->rd", d_hidden.reshape(flat_rows, 2, ff_half), w_in_all)
    d_mid, unit1 = norm_back(d_normed, norm1_gain, centred1, inverse1)
    d_norm1_gain = jnp.sum(d_normed * unit1, axis=0)
    d_norm1_bias = jnp.sum(d_normed, axis=0)
    d_attn = d_mid.astype(bf16)
    d_w_out = dot_to("re,rd->ed", attended_flat, d_attn)
    d_attended = dot_to("rd,ed->re", d_attn, w_out_all).astype(bf16).reshape(attended.shape)

    embed_rows = jnp.transpose(embed_all, (1, 0, 2))
    embed_rows = jnp.concatenate([embed_rows, embed_rows], axis=-1)
    d_query, dk_own, dv_own, dk_ext, dv_ext, small, diag = attend_back(
        full, queries, key_own, value_own, key_ext, value_ext, lanes, attended, d_attended,
        (weight_own, weight_ext), embed_rows, content_all[:, :, None], diagonals.shape[-1],
    )
    aligned = []
    begin = 0
    for block in (rows, rows, mem_rows):
        piece = diag[:, :, begin : begin + block + rows]
        begin += block + rows
        aligned.append(sum(jnp.roll(piece[:, step], -step, axis=-1) for step in range(piece.shape[1])))
    d_rel = jnp.einsum("hl,rl->hr", jnp.concatenate(aligned, -1), hot, precision=highest) * SCALE
    odd = (jnp.arange(heads) % 2)[:, None, None]
    small = jnp.where(odd == 0, small[:, :, :HDIM], small[:, :, HDIM:]) * SCALE
    d_content_bias = small[:, 4]
    d_embed = [small[:, c] + small[:, 2 + c] * seg_all for c in range(2)]
    d_seg_bias = small[:, 2] * embed_all[0] + small[:, 3] * embed_all[1]

    pair_flat = pair.reshape(flat_rows, width)
    d_query_flat = d_query.reshape(flat_rows, width)
    d_wq = dot_to("re,rd->ed", d_query_flat, pair_flat)
    d_wk = dot_to("sej,sjd->ed", dk_own, content) + dot_to("sej,sjd->ed", dk_ext, ext_rows)
    d_wv = dot_to("sej,sjd->ed", dv_own, content) + dot_to("sej,sjd->ed", dv_ext, ext_rows)
    head_small = jnp.concatenate(
        [d_content_bias, d_seg_bias, d_embed[0], d_embed[1], d_rel], axis=1
    ).reshape(2, -1)
    shared = jnp.concatenate([d_norm1_gain, d_norm1_bias, d_norm2_gain, d_norm2_bias, d_b_ffo])
    smalls = jnp.concatenate(
        [jnp.broadcast_to(shared, (2,) + shared.shape), d_b_in.reshape(2, -1), head_small], axis=1
    )
    small_size = smalls.shape[1]
    smalls = jnp.pad(smalls, ((0, 0), (0, -small_size % width)))
    heads_width = width // 2
    proj_sums = sum_rows(
        jnp.concatenate(
            [member.astype(bf16).reshape(2, heads_width, width) for member in (d_wq, d_wk, d_wv, d_w_out)]
            + [smalls.astype(bf16).reshape(2, -1, width)],
            axis=1,
        )
    )

    def back_keys(dk, dv):
        def part(d_rows, weight):
            split = d_rows.reshape(slots, 2, -1, d_rows.shape[-1])
            return dot_to("stej,tde->sjd", split, weight)

        return part(dk, wk) + part(dv, wv)

    d_ext = back_keys(dk_ext, dv_ext).astype(bf16)
    mem_mine = jnp.where(half == 0, d_ext[:, rows : rows + mem_half], d_ext[:, rows + mem_half :])
    mem_away = jnp.where(half == 0, d_ext[:, rows + mem_half :], d_ext[:, rows : rows + mem_half])
    arrived = other_of(jnp.concatenate([d_ext[:, :rows], mem_away], axis=1)).astype(f32)
    d_pair = (
        d_mid + dot_to("rte,tde->rd", d_query_flat.reshape(flat_rows, 2, heads_width), wq)
    ).reshape(slots, 2, rows, width)
    d_content = d_pair[:, 0] + back_keys(dk_own, dv_own) + arrived[:, :rows]
    d_memory = mem_mine.astype(f32) + arrived[:, rows:]

    def take(values_in, at, shape):
        size = 1
        for extent in shape:
            size *= extent
        return values_in[at : at + size].reshape(shape), at + size

    small_sum = proj_sums[4 * heads_width :].reshape(-1)[:small_size]
    at = 0
    vectors = []
    for _ in range(5):
        vector, at = take(small_sum, at, (width,))
        vectors.append(vector)
    sum_b_in, at = take(small_sum, at, (ff_half,))
    per_head_sums, at = take(small_sum, at, (heads_half, 4 * HDIM + NREL))
    d_small = [per_head_sums[:, HDIM * c : HDIM * (c + 1)] for c in range(4)]
    blocks = [proj_sums[heads_width * c : heads_width * (c + 1)] for c in range(4)]
    return (
        outputs[:, 0][None],
        outputs[:, 1][None],
        d_content.astype(bf16)[None],
        d_pair[:, 1].astype(bf16)[None],
        d_memory.astype(bf16)[None],
        blocks[0].T,
        blocks[1].T,
        blocks[2].T,
        blocks[3],
        d_small[0],
        d_small[1],
        jnp.stack([d_small[2], d_small[3]]),
        per_head_sums[:, 4 * HDIM :],
        vectors[0],
        vectors[1],
        ffn_sums[ff_half:].T,
        sum_b_in,
        ffn_sums[:ff_half],
        vectors[4],
        vectors[2],
        vectors[3],
    )


def solution(mesh):
    rows = P("dp", None, "tensor", None)
    columns = P(None, "tensor")
    lead = P("tensor", None)
    group = P("dp", None, None)
    return jax.shard_map(
        per_device,
        mesh=mesh,
        in_specs=(
            rows, rows, rows, rows, rows, columns, columns, columns, lead, lead, lead,
            P(None, "tensor", None), lead, P(), P(), columns, P("tensor"), lead, P(), P(), P(),
            P("dp", None), group, group, group, group,
        ),
        out_specs=(
            rows, rows, rows, rows, rows, columns, columns, columns, lead, lead, lead,
            P(None, "tensor", None), lead, P(), P(), columns, P("tensor"), lead, P(), P(), P(),
        ),
        check_vma=False,
    )
```

time: 1590 us -> 892 us (0.56)
  matrix products: 482 us -> 116 us
  waiting for transfers between devices: 657 us -> 490 us
  blocking collectives: 103 us -> 0 us
  other arithmetic: 149 us -> 59 us
  Pallas kernels: 0 us -> 73.5 us
  loops' own time: 31.2 us -> 0 us
  local copies, waits for them, and re-layouts: 143 us -> 121 us
    dot_general x100 -> x26, matrix products: 482 us -> 116 us  [the longest x24 115 us: dot_to(): return jnp.einsum(equation, left, right, preferred_element_type=f32)]
    psum x1 -> x0, waiting for transfers between devices: 190 us -> none  [per_device(): lax.psum((weight_terms[0], weight_terms[1], weight_terms[2], weight_terms...]
    psum x2 -> x0, blocking collectives: 103 us -> none  [the longest x1 63.4 us: per_device(): lax.psum((weight_terms[0], weight_terms[1], weight_terms[2], weight_terms...]
    pallas_call x0 -> x2, Pallas kernels: none -> 73.5 us  [the longest x1 38.7 us: attend(): pl.pallas_call(attend_kernel, grid_spec=pltpu.PrefetchScalarGridSpec(num_...]
    reduce_sum x28 -> x7, other arithmetic: 74.4 us -> 7.32 us  [the longest x1 3.01 us: per_device(): d_b_ffo = jnp.sum(d_ffn.astype(f32), axis=0)]
    sub x5 -> x3, other arithmetic: 38.6 us -> 0.01 us  [the longest x1 0.01 us: head_tables(): dots[1] - dots[0]]
    another operation x4 -> x0, loops' own time: 31.2 us -> none  [the longest x1 29.6 us: per_device(): lax.map(attend_slot_back, (stored['query_pair'], stored['key_rows'], stor...]
    while x109 -> x0, local copies, waits for them, and re-layouts: 27.2 us -> none
  transfers between devices with their start and end apart: 16 -> 13, of which waited for: 12 -> 12; matrix products, arithmetic and copies ran while one was open for 8% -> 19% of each run, Pallas kernels for 0% -> 4%
where the time goes in v1:
time: 892 us; the launch traced here: 880 us
  waiting for transfers between devices  490 us (55%)
  local copies, waits for them, and re-layouts  121 us (14%)
  matrix products  116 us (13%)
  Pallas kernels  73.5 us (8%)
  other arithmetic  59 us (7%)
  between operations  15.6 us (2%)
    reduce_scatter x2, waiting for transfers between devices, sum_rows(): lax.psum_scatter(flat, ('tensor', 'dp'), scatter_dimension=0, tiled=True)  218 us
    all_gather x6, waiting for transfers between devices, gather_rows(): whole = lax.all_gather(piece, ('tensor', 'dp'), axis=0, tiled=True)  208 us
    dot_general x24, matrix products, dot_to(): return jnp.einsum(equation, left, right, preferred_element_type=f32)  115 us
    pallas_call x1, Pallas kernels, attend(): pl.pallas_call(attend_kernel, grid_spec=pltpu.PrefetchScalarGridSpec(num_...  38.7 us
    all_gather x2, waiting for transfers between devices, sum_rows(): return lax.all_gather(piece, 'dp', axis=0, tiled=True)[:rows].astype(f32)  36.9 us
    pallas_call x1, Pallas kernels, attend_back(): pl.pallas_call(attend_back_kernel, grid_spec=pltpu.PrefetchScalarGridSpec...  34.9 us
    ppermute x3, waiting for transfers between devices, other_of(): lax.ppermute(values_in, 'tensor', [(i, (i + 1) % size) for i in range(siz...  27.2 us
    unnamed x131, local copies, waits for them, and re-layouts  23.1 us
  transfers between devices with their start and end apart: 13, of which 12 were waited for; matrix products, arithmetic and copies ran while one was open for 19% of the time, Pallas kernels for 4%

profile of v1, /device:TPU:0, one launch (start us, length us, event | category | flops | bytes accessed | tf_op | source)
XLA Modules:
  0.0 880.4 jit_solution(7262126340322660383)
XLA Ops:
  16.5 3.0 collective-permute-start.1
  19.5 2.6 pad_maximum_fusion.4
  41.4 2.6 fusion.27
  46.7 8.7 collective-permute-done
  59.7 9.5 %all-gather.13.cloned.1.call-done = bf16[1536,384]{1,0:T(8,128)(2,1)} async-done(((bf16[48,384]{1,0:T(8,128)(2,1)}), bf16[1536,384]{1,0:T(8,128)(2,1)}) %all-gather.13.cloned.1.call-update) | async-done | bytes 1179664 | tf_op jit(solution)/shard_map/all_gather | solution.py:436
  69.2 3.2 fusion.14
  72.4 3.0 copy.261
  75.4 3.1 convert_element_type.413.vo_ref
  78.6 47.0 %all-gather.11.cloned.1.call-done = bf16[1536,384]{1,0:T(8,128)(2,1)} async-done(((bf16[48,384]{1,0:T(8,128)(2,1)}), bf16[1536,384]{1,0:T(8,128)(2,1)}) %all-gather.11.cloned.1.call-update) | async-done | bytes 1179664 | tf_op jit(solution)/shard_map/all_gather | solution.py:436
  125.6 3.2 fusion.13
  128.8 3.0 copy.259
  131.8 3.1 convert_element_type.410.ko_ref
  139.7 42.3 %all-gather.9.cloned.1.call-done = bf16[1536,384]{1,0:T(8,128)(2,1)} async-done(((bf16[48,384]{1,0:T(8,128)(2,1)}), bf16[1536,384]{1,0:T(8,128)(2,1)}) %all-gather.9.cloned.1.call-update) | async-done | bytes 1179664 | tf_op jit(solution)/shard_map/all_gather | solution.py:436
  181.9 2.5 copy.257
  184.5 4.5 convolution_convert_fusion.5
  189.0 3.1 convolution_convert_fusion.2.ve_ref
  192.1 3.0 convolution_convert_fusion.3.ke_ref
  195.9 38.7 %attend.1 = (bf16[2,2,256,768]{3,2,1,0:T(8,128)(2,1)}, bf16[2,2,12,256,256]{4,3,2,1,0:T(8,128)(2,1)}, bf16[2,2,12,256,640]{4,3,2,1,0:T(8,128)(2,1)}) custom-call(s32[2]{0:T(128)} %compare_convert_fusion.full_ref, bf16[2,2,256,768]{3,2,1,0:T(8,128)(2,1)} %bitcast.352, bf16[2,256,768]{2,1,0:T(8,128)(2,1)} %convert_element_type.410.ko_ref, ...), custom_call_target="tpu_custom_call" | custom-call | tf_op jit(solution)/shard_map/attend/pallas_call | solution.py:262
  234.6 3.0 all-gather.15.cloned.1.call-done
  237.6 3.8 fusion.113
  243.6 59.3 %all-gather.17.cloned.1.call-done = bf16[1536,1536]{1,0:T(8,128)(2,1)} async-done(((bf16[48,1536]{1,0:T(8,128)(2,1)}), bf16[1536,1536]{1,0:T(8,128)(2,1)}) %all-gather.17.cloned.1.call-update) | async-done | bytes 4718608 | tf_op jit(solution)/shard_map/all_gather | solution.py:436
  302.9 6.6 copy.266
  309.5 11.3 %fusion.105 = f32[1024,3072]{1,0:T(8,128)} fusion(bf16[3072,768]{1,0:T(8,128)(2,1)} %bitcast.364, f32[1024,768]{1,0:T(8,128)} %copy-done.2, f32[768]{0:T(1024)S(1)} %copy-done.54, f32[768]{0:T(1024)S(1)} %copy-done.43, f32[1024]{0:T(1024)S(1)} %add_rsqrt_fusion.1, f32[1024]{0:T(1024)S(1)} %broadcast_multiply_fusion.6), kind=kOutput, calls=%fused_computation.336 | convolution fusion | flops 4835770368 | bytes 20461568 | tf_op jit(solution)/shard_map/rd,tdf->rtf/dot_general | solution.py:475
  320.9 46.7 %all-gather.19.cloned.1.call-done = bf16[3072,768]{1,0:T(8,128)(2,1)} async-done(((bf16[96,768]{1,0:T(8,128)(2,1)}), bf16[3072,768]{1,0:T(8,128)(2,1)}) %all-gather.19.cloned.1.call-update) | async-done | bytes 4718608 | tf_op jit(solution)/shard_map/all_gather | solution.py:436
  367.6 12.9 %fusion.114 = (f32[1024]{0:T(1024)S(1)}, f32[1024,768]{1,0:T(8,128)S(1)}) fusion(f32[768]{0:T(1024)S(1)} %copy-done.53, bf16[3072,768]{1,0:T(8,128)(2,1)} %all-gather.19.cloned.1.call-done, f32[1024,3072]{1,0:T(8,128)} %fusion.105, f32[3072]{0:T(1024)S(1)} %pad_maximum_fusion.10, f32[768]{0:T(1024)S(1)} %copy-done.54, f32[768]{0:T(1024)S(1)} %copy-done.43, ...), kind=kOutput, calls=%fused_computation.341 | convolution fusion | flops 4868799488 | bytes 23626752 | tf_op jit(solution)/shard_map/rf,fd->rd/dot_general | solution.py:475
  382.5 3.0 convert_reduce_fusion
  385.6 17.6 %fusion.115 = (bf16[3072]{0:T(1024)(128)(2,1)}, bf16[1024,3072]{1,0:T(8,128)(2,1)}) fusion(f32[1024,3072]{1,0:T(8,128)} %fusion.105, f32[3072]{0:T(1024)S(1)} %pad_maximum_fusion.10, bf16[3072,768]{1,0:T(8,128)(2,1)} %all-gather.19.cloned.1.call-done, f32[1024,768]{1,0:T(8,128)S(1)} %get-tuple-element.162), kind=kOutput, calls=%fused_computation.342 | convolution fusion | flops 4895536128 | bytes 26757120 | tf_op jit(solution)/shard_map/rd,fd->rf/dot_general | solution.py:475
  403.2 9.3 %multiply_reduce_fusion = (f32[768]{0:T(1024)}, f32[1024]{0:T(1024)S(1)}, f32[1024]{0:T(1024)S(1)}, f32[768]{0:T(1024)}, f32[1024,768]{1,0:T(8,128)S(1)}) fusion(f32[1024,768]{1,0:T(8,128)S(1)} %copy-done.3, f32[1024]{0:T(1024)S(1)} %add_rsqrt_fusion.1, f32[1024]{0:T(1024)S(1)} %broadcast_multiply_fusion.6, f32[768]{0:T(1024)S(1)} %copy-done.43, ...), kind=kOutput, calls=%fused_computation.20 | convolution fusion | flops 4839698432 | bytes 20472832 | tf_op jit(solution)/shard_map/rtf,tdf->rd/dot_general | solution.py:475
  413.7 2.6 convolution_convert_fusion.4
  416.4 34.9 %attend_back.1 = (bf16[2,2,256,768]{3,2,1,0:T(8,128)(2,1)}, bf16[2,768,256]{2,1,0:T(8,128)(2,1)}, bf16[2,768,256]{2,1,0:T(8,128)(2,1)}, bf16[2,768,640]{2,1,0:T(...) custom-call(s32[2]{0:T(128)} %compare_convert_fusion.full_ref, ...), custom_call_target="tpu_custom_call" | custom-call | tf_op jit(solution)/shard_map/attend_back/pallas_call | solution.py:395
  474.5 2.5 convolution_convert_fusion.6
  495.9 3.4 bitcast_convert_fusion
  507.4 2.7 pad.10
  510.8 9.0 %convolution_convert_fusion = bf16[3072,768]{1,0:T(8,128)(2,1)S(1)} fusion(bf16[1024,3072]{1,0:T(8,128)(2,1)} %get-tuple-element.250, f32[1024,768]{1,0:T(8,128)} %copy-done.2, f32[768]{0:T(1024)S(1)} %copy-done.55, f32[768]{0:T(1024)S(1)} %copy-done.44, f32[1024]{0:T(1024)S(1)} %copy-done.38, f32[1024]{0:T(1024)S(1)} %broadcast_multiply_fusion.6), kind=kOutput, calls=%fused_computation.8 | convolution fusion | flops 4838129664 | bytes 14170112 | tf_op jit(solution)/shard_map/rf,rd->fd/dot_general | solution.py:475
  519.8 11.0 %convolution_convert_fusion.1 = bf16[3072,768]{1,0:T(8,128)(2,1)S(1)} fusion(f32[1024,768]{1,0:T(8,128)S(1)} %copy-done.16, f32[1024,3072]{1,0:T(8,128)} %fusion.105, f32[3072]{0:T(1024)S(1)} %copy-done.40), kind=kOutput, calls=%fused_computation.9 | convolution fusion | flops 4866441216 | bytes 20459520 | tf_op jit(solution)/shard_map/rf,rd->fd/dot_general | solution.py:475
  530.8 10.1 %pad_maximum_fusion = bf16[2,3072,768]{2,1,0:T(8,128)(2,1)} fusion(bf16[2,1536,768]{2,1,0:T(8,128)(2,1)S(1)} %bitcast.365, bf16[2,1536,768]{2,1,0:T(8,128)(2,1)S(1)} %bitcast.366), kind=kLoop, calls=%fused_computation.4 | loop fusion | flops 18874368 | bytes 18874368 | tf_op jit(solution)/shard_map/concatenate | solution.py:576
  541.0 76.9 %reduce-scatter.3.cloned.1.call-done = bf16[104,768]{1,0:T(8,128)(2,1)} async-done(((bf16[3328,768]{1,0:T(8,128)(2,1)}), bf16[104,768]{1,0:T(8,128)(2,1)}) %reduce-scatter.3.cloned.1.call-update) | async-done | bytes 159760 | tf_op jit(solution)/shard_map/reduce_scatter | solution.py:447
  618.2 141.0 %reduce-scatter.5.cloned.1.call-done = bf16[192,768]{1,0:T(8,128)(2,1)} async-done(((bf16[6144,768]{1,0:T(8,128)(2,1)}), bf16[192,768]{1,0:T(8,128)(2,1)}) %reduce-scatter.5.cloned.1.call-update) | async-done | bytes 294928 | tf_op jit(solution)/shard_map/reduce_scatter | solution.py:447
  759.2 3.8 fusion.117
  768.9 4.4 reshape_reshape.3
  773.2 2.8 slice_bitcast_fusion.5
  779.3 18.5 %collective-permute-done.2 = bf16[2,448,768]{2,1,0:T(8,128)(2,1)} collective-permute-done((bf16[2,448,768]{2,1,0:T(8,128)(2,1)}, bf16[2,448,768]{2,1,0:T(8,128)(2,1)}, u32[]{:S(2)}, u32[]{:S(2)}) %collective-permute-start.2) | collective-permute-done | bytes 1376288 | tf_op jit(solution)/shard_map/ppermute | solution.py:423
  803.1 4.2 slice_convert_fusion
  811.5 4.0 fusion.110
  821.2 36.0 %all-gather.23.cloned.1.call-done = bf16[3072,768]{1,0:T(8,128)(2,1)} async-done(((bf16[192,768]{1,0:T(8,128)(2,1)}), bf16[3072,768]{1,0:T(8,128)(2,1)}) %all-gather.23.cloned.1.call-update) | async-done | bytes 4718608 | tf_op jit(solution)/shard_map/all_gather | solution.py:448
  857.2 3.1 convert_element_type.478
  862.7 6.2 copy.310
  868.9 4.2 slice.660
  (340 shorter events, 124.1 us)
Async XLA Ops:
  7.2 6.1 copy-start
  7.2 16.6 %copy-start.47 = (s32[1,2]{1,0:T(1,128)S(1)}, s32[1,2]{1,0:T(1,128)}, u32[]{:S(2)}) copy-start(s32[1,2]{1,0:T(1,128)} %param.47) | copy-start | bytes 28
  7.2 17.2 %copy-start.46 = (s32[1,2,384]{2,1,0:T(2,128)S(1)}, s32[1,2,384]{2,1,0:T(2,128)}, u32[]{:S(2)}) copy-start(s32[1,2,384]{2,1,0:T(2,128)} %param.50) | copy-start | bytes 9220
  7.2 17.2 %copy-start.41 = (s32[1,2,512]{2,1,0:T(2,128)S(1)}, s32[1,2,512]{2,1,0:T(2,128)}, u32[]{:S(2)}) copy-start(s32[1,2,512]{2,1,0:T(2,128)} %param.49) | copy-start | bytes 12292
  7.2 17.3 %copy-start.45 = (s32[1,2,512]{2,1,0:T(2,128)S(1)}, s32[1,2,512]{2,1,0:T(2,128)}, u32[]{:S(2)}) copy-start(s32[1,2,512]{2,1,0:T(2,128)} %param.51) | copy-start | bytes 12292
  7.2 17.6 %copy-start.48 = (s32[1,2,8]{2,1,0:T(2,128)S(1)}, s32[1,2,8]{2,1,0:T(2,128)}, u32[]{:S(2)}) copy-start(s32[1,2,8]{2,1,0:T(2,128)} %param.48) | copy-start | bytes 196
  7.3 61.9 %all-gather.13.cloned.1.call-start = ((), (), s32[]{:S(2)}) async-start(), calls=%async_computation.4 | async-start | bytes 1216512 | tf_op jit(solution)/shard_map/all_gather | solution.py:436
  8.9 116.7 %all-gather.11.cloned.1.call-start = ((), (), s32[]{:S(2)}) async-start(), calls=%async_computation.3 | async-start | bytes 1216512 | tf_op jit(solution)/shard_map/all_gather | solution.py:436
  10.3 171.6 %all-gather.9.cloned.1.call-start = ((), (), s32[]{:S(2)}) async-start(), calls=%async_computation.2 | async-start | bytes 1216512 | tf_op jit(solution)/shard_map/all_gather | solution.py:436
  11.8 225.8 %all-gather.15.cloned.1.call-start = ((), (), s32[]{:S(2)}) async-start(), calls=%async_computation.5 | async-start | bytes 1216512 | tf_op jit(solution)/shard_map/all_gather | solution.py:436
  13.3 289.6 %all-gather.17.cloned.1.call-start = ((), (), s32[]{:S(2)}) async-start(), calls=%async_computation.6 | async-start | bytes 4866048 | tf_op jit(solution)/shard_map/all_gather | solution.py:436
  14.0 353.6 %all-gather.19.cloned.1.call-start = ((), (), s32[]{:S(2)}) async-start(), calls=%async_computation.7 | async-start | bytes 4866048 | tf_op jit(solution)/shard_map/all_gather | solution.py:436
  16.5 19.8 %collective-permute-start.1 = (f32[3264]{0:T(1024)S(1)}, f32[3264]{0:T(1024)S(1)}, u32[]{:S(2)}, u32[]{:S(2)}) collective-permute-start(f32[3264]{0:T(1024)S(1)} %pad_maximum_fusion.8), channel_id=1, source_target_pairs={{0,1},{1,0},{2,3},{3,2},{4,5},{5,4},{6,7},{7,6},{8,9},{9,8},{10,11... | collective-permute-start | bytes 39176 | tf_op jit(solution)/shard_map/ppermute | solution.py:423
  19.5 9.9 %copy-start.4 = (bf16[1,2,256,768]{3,2,1,0:T(8,128)(2,1)S(1)}, bf16[1,2,256,768]{3,2,1,0:T(8,128)(2,1)}, u32[]{:S(2)}) copy-start(bf16[1,2,256,768]{3,2,1,0:T(8,128)(2,1)} %param.26) | copy-start | bytes 2359300
  19.5 9.9 %copy-start.27 = (bf16[1,2,256,768]{3,2,1,0:T(8,128)(2,1)S(1)}, bf16[1,2,256,768]{3,2,1,0:T(8,128)(2,1)}, u32[]{:S(2)}) copy-start(bf16[1,2,256,768]{3,2,1,0:T(8,128)(2,1)} %param.27) | copy-start | bytes 2359300
  22.1 33.3 %collective-permute-start = (bf16[2,448,768]{2,1,0:T(8,128)(2,1)}, bf16[2,448,768]{2,1,0:T(8,128)(2,1)}, u32[]{:S(2)}, u32[]{:S(2)}) collective-permute-start(bf16[2,448,768]{2,1,0:T(8,128)(2,1)} %pad_maximum_fusion.4), channel_id=1, source_target_pairs={{0,1},{1,0},{2,3},{3,2},{4,5},{5,4},{6,7},{7,6},{8,9},{9,8},{10,11... | collective-permute-start | bytes 4128776 | tf_op jit(solution)/shard_map/ppermute | solution.py:423
  23.7 594.2 %reduce-scatter.3.cloned.1.call-start = ((), (), s32[]{:S(2)}) async-start(), calls=%async_computation.8 | async-start | bytes 5271552 | tf_op jit(solution)/shard_map/reduce_scatter | solution.py:447
  25.7 4.9 copy-start.13
  25.8 4.9 copy-start.14
  32.6 6.1 copy-start.35
  34.1 4.5 copy-start.36
  40.6 345.0 %copy-start.39 = (f32[3072]{0:T(1024)}, f32[3072]{0:T(1024)S(1)}, u32[]{:S(2)}) copy-start(f32[3072]{0:T(1024)S(1)} %pad_maximum_fusion.10) | copy-start | bytes 36868
  45.1 12.3 %copy-start.19 = (bf16[1,2,192,768]{3,2,1,0:T(8,128)(2,1)S(1)}, bf16[1,2,192,768]{3,2,1,0:T(8,128)(2,1)}, u32[]{:S(2)}) copy-start(bf16[1,2,192,768]{3,2,1,0:T(8,128)(2,1)} %param.28) | copy-start | bytes 1769476
  184.5 4.5 copy-start.24
  184.5 4.5 copy-start.25
  184.5 4.5 copy-start.30
  184.5 4.5 copy-start.32
  243.6 168.8 %copy-start.37 = (f32[1024]{0:T(1024)}, f32[1024]{0:T(1024)S(1)}, u32[]{:S(2)}) copy-start(f32[1024]{0:T(1024)S(1)} %add_rsqrt_fusion.1) | copy-start | bytes 12292
  302.9 6.6 copy-start.43
  302.9 6.6 copy-start.54
  309.5 58.0 %copy-start.53 = (f32[768]{0:T(1024)S(1)}, f32[768]{0:T(1024)}, u32[]{:S(2)}) copy-start(f32[768]{0:T(1024)} %param.44) | copy-start | bytes 9220
  382.5 20.7 %slice-start = ((s8[4718592]{0:T(1024)(128)(4,1)}), s8[4194304]{0:T(1024)(128)(4,1)S(1)}, s32[]{:S(2)}) async-start(s8[4718592]{0:T(1024)(128)(4,1)} %bitcast.361), calls=%async_computation.12 | async-start | bytes 8388608
  385.6 17.6 %copy-start.15 = (f32[1024,768]{1,0:T(8,128)}, f32[1024,768]{1,0:T(8,128)S(1)}, u32[]{:S(2)}) copy-start(f32[1024,768]{1,0:T(8,128)S(1)} %get-tuple-element.162) | copy-start | bytes 9437188
  385.6 17.6 %copy-start.3 = (f32[1024,768]{1,0:T(8,128)S(1)}, f32[1024,768]{1,0:T(8,128)}, u32[]{:S(2)}) copy-start(f32[1024,768]{1,0:T(8,128)} %copy-done.2) | copy-start | bytes 9437188
  385.6 17.6 %slice-start.1 = ((s8[4718592]{0:T(1024)(128)(4,1)}), s8[524288]{0:T(1024)(128)(4,1)S(1)}, s32[]{:S(2)}) async-start(s8[4718592]{0:T(1024)(128)(4,1)} %bitcast.361), calls=%async_computation.13 | async-start | bytes 1048576
  451.2 23.3 %copy-start.20 = (bf16[2,2,256,768]{3,2,1,0:T(8,128)(2,1)S(1)}, bf16[2,2,256,768]{3,2,1,0:T(8,128)(2,1)}, u32[]{:S(2)}) copy-start(bf16[2,2,256,768]{3,2,1,0:T(8,128)(2,1)} %get-tuple-element.31.a_ref) | copy-start | bytes 4718596
  454.2 4.2 copy-start.12
  510.1 9.7 %copy-start.40 = (f32[3072]{0:T(1024)S(1)}, f32[3072]{0:T(1024)}, u32[]{:S(2)}) copy-start(f32[3072]{0:T(1024)} %copy-done.39) | copy-start | bytes 36868
  510.1 249.1 %reduce-scatter.5.cloned.1.call-start = ((), (), s32[]{:S(2)}) async-start(), calls=%async_computation.10 | async-start | bytes 9732096 | tf_op jit(solution)/shard_map/reduce_scatter | solution.py:447
  510.8 9.1 %copy-start.16 = (f32[1024,768]{1,0:T(8,128)S(1)}, f32[1024,768]{1,0:T(8,128)}, u32[]{:S(2)}) copy-start(f32[1024,768]{1,0:T(8,128)} %copy-done.15) | copy-start | bytes 9437188
  540.9 262.2 %all-gather.21.cloned.1.call-start = ((), (), s32[]{:S(2)}) async-start(), calls=%async_computation.9 | async-start | bytes 2715648 | tf_op jit(solution)/shard_map/all_gather | solution.py:448
  617.9 239.3 %all-gather.23.cloned.1.call-start = ((), (), s32[]{:S(2)}) async-start(), calls=%async_computation.11 | async-start | bytes 5013504 | tf_op jit(solution)/shard_map/all_gather | solution.py:448
  759.2 3.8 copy-start.10
  767.4 30.5 %collective-permute-start.2 = (bf16[2,448,768]{2,1,0:T(8,128)(2,1)}, bf16[2,448,768]{2,1,0:T(8,128)(2,1)}, u32[]{:S(2)}, u32[]{:S(2)}) collective-permute-start(bf16[2,448,768]{2,1,0:T(8,128)(2,1)} %pad_maximum_fusion.5), channel_id=1, source_target_pairs={{0,1},{1,0},{2,3},{3,2},{4,5},{5,4},{6,7},{7,6},{8,9},{9,8},{10,11... | collective-permute-start | bytes 4128776 | tf_op jit(solution)/shard_map/ppermute | solution.py:423
  778.5 21.0 %copy-start.8 = (bf16[2,640,768]{2,1,0:T(8,128)(2,1)S(1)}, bf16[2,640,768]{2,1,0:T(8,128)(2,1)}, u32[]{:S(2)}) copy-start(bf16[2,640,768]{2,1,0:T(8,128)(2,1)} %copy-done.7) | copy-start | bytes 5898244
  779.3 21.2 %copy-start.11 = (bf16[1536,384]{1,0:T(8,128)(2,1)S(1)}, bf16[1536,384]{1,0:T(8,128)(2,1)}, u32[]{:S(2)}) copy-start(bf16[1536,384]{1,0:T(8,128)(2,1)} %all-gather.13.cloned.1.call-done) | copy-start | bytes 3538948
  779.3 21.2 %copy-start.18 = (bf16[2,768,256]{2,1,0:T(8,128)(2,1)S(1)}, bf16[2,768,256]{2,1,0:T(8,128)(2,1)}, u32[]{:S(2)}) copy-start(bf16[2,768,256]{2,1,0:T(8,128)(2,1)} %get-tuple-element.36) | copy-start | bytes 2359300
  862.7 10.4 %copy-start.1 = (bf16[768,1536]{1,0:T(8,128)(2,1)S(1)}, bf16[768,1536]{1,0:T(8,128)(2,1)}, u32[]{:S(2)}) copy-start(bf16[768,1536]{1,0:T(8,128)(2,1)} %param.41) | copy-start | bytes 7077892
  (23 other events, 44.3 us)
Sparse Core Ops, SparseCore 0:
  11.5 57.6 all-gather.12
  72.7 52.8 all-gather.10
  129.0 52.8 all-gather.8
  184.7 52.8 all-gather.14
  240.4 62.4 all-gather.16
  305.7 61.8 all-gather.18
  510.2 107.6 reduce-scatter.2
  623.8 135.3 reduce-scatter.4
  761.3 41.7 all-gather.20
  805.3 51.8 all-gather.22
